TPU v7x, 32 devices: a whole 2x2x4 slice. The times are simulated.
32 devices in a mesh: line: 8 (over z, y), bus: 4 (over x, core).
Axes of the slice: x: 2, y: 2, z: 4, core: 2. Of those that a mesh axis runs over, the one named last changes fastest.
Arguments:
- clearness: float32 [192, 8192], P(None, ('line', 'bus')), may hold values from 0.05 to 0.8
- cos_zenith: float32 [192, 8192], P(None, ('line', 'bus')), may hold values from 0.05 to 1
- sun_azimuth: float32 [192, 8192], P(None, ('line', 'bus')), may hold values from -3.140625 to 3.140625
- dirint_cell: int32 [192, 8192], P(None, ('line', 'bus')), may hold values from 0 to 1259
- sky_bin: int32 [192, 8192], P(None, ('line', 'bus')), may hold values from 0 to 7
- dirint_coef: float32 [1260], replicated, may hold values from 0.5 to 1.5
- perez_coef: float32 [6, 8], replicated, may hold values from -0.3 to 0.6
- tilt_class: int32 [8192], P(('line', 'bus')), may hold values from 0 to 7
- azimuth_class: int32 [8192], P(('line', 'bus')), may hold values from 0 to 11
- tilt_table: float32 [8], replicated, may hold values from 0 to 1
- azimuth_table: float32 [12], replicated, may hold values from -3.140625 to 3.140625
- capacity: float32 [8192], P(('line', 'bus')), may hold values from 0.2 to 2
- site_bus: int32 [8192], P(('line', 'bus')), may hold values from 0 to 70143, as said below
- transfer_factors: bfloat16 [16000, 70144], P('line', 'bus'), may hold values from -0.0234375 to 0.0234375
Outputs:
- flows: float32 [16000, 192], P('line', 'bus')
Inputs may be any that keep to these rules, and one draw needn't show every extreme that they name: `site_bus`: bus b lies in group b // 2192. In every aligned block of 256 sites at most 16 sites connect to buses of one group, and one group receives exactly 16 sites from every block.
All inputs are finite; a program needn't handle non-finite values.
Results may differ from a plain program's by a relative error of at most 0.0034.
Values may be sent and summed in bfloat16 or wider, within the bound.
No kernel may reach another device: no remote copies, remote signals or barrier semaphores. Data moves between devices by JAX's collectives and lax.ppermute only.
A program may use at most 128 MiB of HBM per device.

v0:
```python
import math

import jax
import jax.numpy as jnp
from jax import lax
from jax.sharding import PartitionSpec as P

BUSES = 70144
TILTS = 8
AZIMS = 12


solar_constant = 1367.0
albedo = 0.2
cos_limit = 0.08716
row_width = 36


def pick_table(classes, table, count):
    picked = jnp.zeros(classes.shape, jnp.float32)
    for entry in range(count):
        picked = jnp.where(classes == entry, table[entry], picked)
    return picked


def dirint_lookup(cell, dirint_coef):
    row_count = dirint_coef.shape[0] // row_width
    table = dirint_coef.reshape(row_count, row_width)
    flat_cell = cell.reshape(-1)
    upper = flat_cell // row_width
    lower = flat_cell % row_width
    row_pick = (upper[:, None] == jnp.arange(row_count, dtype=jnp.int32)[None, :]).astype(
        jnp.float32
    )
    rows = jnp.dot(
        row_pick, table, precision=lax.Precision.HIGHEST, preferred_element_type=jnp.float32
    )
    column_hit = lower[:, None] == jnp.arange(row_width, dtype=jnp.int32)[None, :]
    picked = jnp.sum(jnp.where(column_hit, rows, 0.0), axis=1)
    return picked.reshape(cell.shape)


def site_power(
    clear,
    cosz,
    sun_az,
    cell,
    sky,
    tilt_angle,
    array_azimuth,
    site_capacity,
    dirint_coef,
    perez_coef,
):
    global_flat = clear * solar_constant * cosz
    zenith = jnp.arccos(cosz)
    airmass = 1.0 / (cosz + 0.50572 * (96.07995 - zenith * (180.0 / math.pi)) ** (-1.6364))
    clear_beam = (
        0.866 - 0.122 * airmass + 0.0121 * airmass**2 - 0.000653 * airmass**3 + 1.4e-05 * airmass**4
    )
    part_a = 0.512 - 1.56 * clear + 2.286 * clear**2 - 2.222 * clear**3
    part_b = 0.37 + 0.962 * clear
    part_c = -0.28 + 0.932 * clear - 2.048 * clear**2
    beam_index = jnp.maximum(clear_beam - (part_a + part_b * jnp.exp(part_c * airmass)), 0.0)
    direct_normal = solar_constant * beam_index * dirint_lookup(cell, dirint_coef)
    diffuse = jnp.maximum(global_flat - direct_normal * cosz, 0.1 * global_flat)
    brightness = diffuse * airmass / solar_constant
    factors = [jnp.zeros(cosz.shape, jnp.float32) for entry in range(6)]
    for bin_index in range(perez_coef.shape[1]):
        hit = sky == bin_index
        factors = [jnp.where(hit, perez_coef[row, bin_index], factors[row]) for row in range(6)]
    circumsolar = jnp.maximum(0.0, factors[0] + factors[1] * brightness + factors[2] * zenith)
    horizon_term = factors[3] + factors[4] * brightness + factors[5] * zenith
    cos_tilt = jnp.cos(tilt_angle)
    sin_tilt = jnp.sin(tilt_angle)
    cos_incidence = cosz * cos_tilt + jnp.sin(zenith) * sin_tilt * jnp.cos(sun_az - array_azimuth)
    facing = jnp.maximum(cos_incidence, 0.0)
    horizon_cos = jnp.maximum(cosz, cos_limit)
    sky_part = diffuse * (
        (1.0 - circumsolar) * (1.0 + cos_tilt) * 0.5
        + circumsolar * facing / horizon_cos
        + horizon_term * sin_tilt
    )
    plane = direct_normal * facing + sky_part + albedo * global_flat * (1.0 - cos_tilt) * 0.5
    return (site_capacity * plane / 1000.0).astype(jnp.bfloat16)


def per_device(
    clearness,
    cos_zenith,
    sun_azimuth,
    dirint_cell,
    sky_bin,
    dirint_coef,
    perez_coef,
    tilt_class,
    azimuth_class,
    tilt_table,
    azimuth_table,
    capacity,
    site_bus,
    transfer_factors,
):
    line_count = lax.axis_size("line")
    bus_count = lax.axis_size("bus")
    owners = line_count * bus_count
    n_hours, n_sites = clearness.shape
    group_buses = BUSES // owners
    slots_each = max(2, 2 * n_sites // owners)
    tilt_angle = pick_table(tilt_class, tilt_table, TILTS)
    array_azimuth = pick_table(azimuth_class, azimuth_table, AZIMS)
    power = site_power(
        clearness,
        cos_zenith,
        sun_azimuth,
        dirint_cell,
        sky_bin,
        tilt_angle,
        array_azimuth,
        capacity,
        dirint_coef,
        perez_coef,
    )
    group_index = site_bus // group_buses
    target = group_index % line_count * bus_count + group_index // line_count
    local_bus = site_bus % group_buses
    one_hot = (target[:, None] == jnp.arange(owners, dtype=jnp.int32)[None, :]).astype(jnp.int32)
    position = jnp.sum(one_hot * (jnp.cumsum(one_hot, axis=0) - 1), axis=1)
    slot_index = target * slots_each + position
    outgoing = jnp.zeros((n_hours, owners * slots_each), jnp.bfloat16).at[:, slot_index].set(power)
    labels = jnp.zeros((1, owners * slots_each), jnp.int32).at[0, slot_index].set(local_bus)
    arrived, bus_tags = (
        lax.all_to_all(outgoing, ("line", "bus"), split_axis=1, concat_axis=1, tiled=True),
        lax.all_to_all(labels, ("line", "bus"), split_axis=1, concat_axis=1, tiled=True),
    )
    bus_tags = bus_tags.reshape(owners * slots_each)
    member = (bus_tags[:, None] == jnp.arange(group_buses, dtype=jnp.int32)[None, :]).astype(
        jnp.bfloat16
    )
    injection = jnp.einsum("hr,rb->bh", arrived, member, preferred_element_type=jnp.float32).astype(
        jnp.bfloat16
    )
    partial_flows = jnp.dot(
        transfer_factors,
        lax.all_gather(injection, "line", axis=0, tiled=True),
        preferred_element_type=jnp.float32,
    )
    return lax.psum_scatter(partial_flows, "bus", scatter_dimension=1, tiled=True)


def solution(mesh):
    in_specs = (
        P(None, ("line", "bus")),
        P(None, ("line", "bus")),
        P(None, ("line", "bus")),
        P(None, ("line", "bus")),
        P(None, ("line", "bus")),
        P(),
        P(),
        P(("line", "bus")),
        P(("line", "bus")),
        P(),
        P(),
        P(("line", "bus")),
        P(("line", "bus")),
        P("line", "bus"),
    )
    out_specs = P("line", "bus")
    return jax.shard_map(
        per_device, mesh=mesh, in_specs=in_specs, out_specs=out_specs, check_vma=False
    )
```

profile of v0, /device:TPU:0, one launch (start us, length us, event | category | flops | bytes accessed | tf_op | source)
XLA Modules:
  0.0 296.3 jit_solution(16229938110226175644)
XLA Ops:
  6.6 0.8 and_select_fusion
  8.3 1.4 scatter_custom_fusion
  10.4 7.3 %all-to-all-start = ((s32[1,32,16]{2,0,1:T(1,128)}), s32[1,32,16]{2,0,1:T(1,128)S(1)}, u32[]{:S(2)}, u32[]{:S(2)}) async-start(s32[1,32,16]{2,0,1:T(1,128)} %bitcast.2), calls=%async_computation | async-start | bytes 32768 | tf_op jit(solution)/shard_map/all_to_all | solution.py:134
  17.7 1.7 fusion.36
  19.4 2.1 fusion.34
  21.5 2.1 fusion.35
  23.6 1.0 sign_compare_fusion
  24.6 1.0 remainder_bitcast_fusion
  25.6 1.6 fusion.38
  27.2 5.7 %fusion.33 = (f32[256]{0:T(256)S(1)}, f32[256]{0:T(256)S(1)}) fusion(f32[]{:T(128)} %bitcast.10, s32[256]{0:T(256)} %param.21, f32[]{:T(128)} %bitcast.9, f32[]{:T(128)} %bitcast.8, f32[]{:T(128)} %bitcast.7, f32[]{:T(128)} %bitcast.6, f32[]{:T(128)} %bitcast.5, f32[]{:T(128)} %bitcast.4, f32[]{:T(128)} %bitcast.3), kind=kLoop, calls=%fused_computation.89 | loop fusion | flops 4096 | bytes 3104 | tf_op jit(solution)/shard_map/sin | solution.py:75
  33.0 1.8 fusion.37
  34.8 0.8 reshape.70
  36.0 5.6 %fusion.5 = f32[49152]{0:T(1024)S(1)} fusion(f32[35,36]{1,0:T(8,128)S(1)} %reshape.70, s32[49152]{0:T(1024)S(1)} %get-tuple-element.8, s32[49152]{0:T(1024)S(1)} %get-tuple-element.7), kind=kOutput, calls=%fused_computation.12 | convolution fusion | flops 750157824 | bytes 594864 | tf_op jit(solution)/shard_map/dot_general | solution.py:35
  41.7 7.5 %broadcast_add_fusion = (f32[256]{0:T(256)S(1)}, f32[256]{0:T(256)S(1)}, f32[256]{0:T(256)S(1)}) fusion(f32[256]{0:T(256)S(1)} %cos.6, f32[]{:T(128)} %bitcast.22, s32[256]{0:T(256)S(1)} %copy-done.4, f32[]{:T(128)} %bitcast.21, f32[]{:T(128)} %bitcast.20, f32[]{:T(128)} %bitcast.19, f32[]{:T(128)} %bitcast.18, f32[]{:T(128)} %bitcast.17, f32[]{:T(128)} %bitcast.16, ...), kind=kLoop, calls=%fused_computation.88 | loop fusion | flops 6912 | bytes 5168 | tf_op jit(solution)/shard_map/add | solution.py:80
  49.3 32.6 %fusion.25 = bf16[256,192]{0,1:T(8,128)(2,1)S(1)} fusion(f32[256]{0:T(256)S(1)} %get-tuple-element.62, f32[]{:T(128)} %bitcast.70, f32[]{:T(128)} %bitcast.69, f32[]{:T(128)} %bitcast.68, f32[]{:T(128)} %bitcast.67, f32[]{:T(128)} %bitcast.66, f32[]{:T(128)} %bitcast.65, f32[]{:T(128)} %bitcast.64, f32[]{:T(128)} %bitcast.63, f32[]{:T(128)} %bitcast.62, ...), kind=kLoop, calls=%fused_computation.45 | loop fusion | flops 6733824 | bytes 1087680 | tf_op jit(solution)/shard_map/convert_element_type | solution.py:85
  81.9 2.1 scatter_custom_fusion.1
  84.1 5.8 %all-to-all-start.1 = ((bf16[192,32,16]{0,2,1:T(8,128)(2,1)}), bf16[192,32,16]{0,2,1:T(8,128)(2,1)S(1)}, u32[]{:S(2)}, u32[]{:S(2)}) async-start(bf16[192,32,16]{0,2,1:T(8,128)(2,1)} %bitcast.72), calls=%async_computation.1 | async-start | bytes 524288 | tf_op jit(solution)/shard_map/all_to_all | solution.py:133
  91.3 9.2 %all-to-all-done.1 = bf16[192,32,16]{0,2,1:T(8,128)(2,1)S(1)} async-done(((bf16[192,32,16]{0,2,1:T(8,128)(2,1)}), bf16[192,32,16]{0,2,1:T(8,128)(2,1)S(1)}, u32[]{:S(2)}, u32[]{:S(2)}) %all-to-all-start.1) | async-done | bytes 196640 | tf_op jit(solution)/shard_map/all_to_all | solution.py:133
  100.5 2.1 fusion.3
  102.9 106.5 %all-gather.3.cloned.1.call-done = bf16[8,2192,192]{1,2,0:T(8,128)(2,1)} async-done(((bf16[1,2192,192]{1,2,0:T(8,128)(2,1)}), bf16[8,2192,192]{1,2,0:T(8,128)(2,1)}) %all-gather.3.cloned.1.call-update) | async-done | bytes 6733840 | tf_op jit(solution)/shard_map/all_gather | solution.py:145
  209.4 9.8 %copy.26 = bf16[8,2192,192]{1,0,2:T(8,128)(2,1)} copy(bf16[8,2192,192]{1,2,0:T(8,128)(2,1)} %all-gather.3.cloned.1.call-done) | data formatting | bytes 13467648 | tf_op jit(solution)/shard_map/all_gather | solution.py:145
  219.3 12.5 %reshape.97 = bf16[17536,192]{0,1:T(8,128)(2,1)} reshape(bf16[8,2192,192]{1,0,2:T(8,128)(2,1)} %copy.26) | data formatting | bytes 13467648
  231.8 31.1 %convolution_bitcast_fusion = f32[2000,192]{0,1:T(8,128)} fusion(bf16[17536,192]{0,1:T(8,128)(2,1)} %reshape.97, bf16[2000,17536]{1,0:T(8,128)(2,1)} %param.27), kind=kOutput, calls=%fused_computation.10 | convolution fusion | flops 13467648000 | bytes 78413824 | tf_op jit(solution)/shard_map/dot_general | solution.py:143
  262.9 26.5 %reduce-scatter.2.cloned.1.call-done = f32[2000,48]{0,1:T(8,128)} async-done(((f32[2000,192]{0,1:T(8,128)}), f32[2000,48]{0,1:T(8,128)}) %reduce-scatter.2.cloned.1.call-update) | async-done | bytes 384016 | tf_op jit(solution)/shard_map/reduce_scatter | solution.py:148
  (35 shorter events, 3.8 us)
Async XLA Ops:
  6.5 35.2 %copy-start.4 = (s32[256]{0:T(256)S(1)}, s32[256]{0:T(256)}, u32[]{:S(2)}) copy-start(s32[256]{0:T(256)} %param.22) | copy-start | bytes 3076
  6.5 42.7 %copy-start.5 = (f32[256]{0:T(256)S(1)}, f32[256]{0:T(256)}, u32[]{:S(2)}) copy-start(f32[256]{0:T(256)} %param.25) | copy-start | bytes 3076
  6.5 42.7 %copy-start.1 = (s32[192,256]{1,0:T(8,128)S(1)}, s32[192,256]{1,0:T(8,128)}, u32[]{:S(2)}) copy-start(s32[192,256]{1,0:T(8,128)} %param.18) | copy-start | bytes 589828
  6.5 42.7 %copy-start.3 = (f32[192,256]{1,0:T(8,128)S(1)}, f32[192,256]{1,0:T(8,128)}, u32[]{:S(2)}) copy-start(f32[192,256]{1,0:T(8,128)} %param.16) | copy-start | bytes 589828
  6.5 42.7 %copy-start = (f32[192,256]{1,0:T(8,128)S(1)}, f32[192,256]{1,0:T(8,128)}, u32[]{:S(2)}) copy-start(f32[192,256]{1,0:T(8,128)} %param.15) | copy-start | bytes 589828
  6.5 42.7 %copy-start.2 = (f32[192,256]{1,0:T(8,128)S(1)}, f32[192,256]{1,0:T(8,128)}, u32[]{:S(2)}) copy-start(f32[192,256]{1,0:T(8,128)} %param.14) | copy-start | bytes 589828
  10.4 73.7 %all-to-all-start = ((s32[1,32,16]{2,0,1:T(1,128)}), s32[1,32,16]{2,0,1:T(1,128)S(1)}, u32[]{:S(2)}, u32[]{:S(2)}) async-start(s32[1,32,16]{2,0,1:T(1,128)} %bitcast.2), calls=%async_computation | async-start | bytes 32768 | tf_op jit(solution)/shard_map/all_to_all | solution.py:134
  84.1 16.4 %all-to-all-start.1 = ((bf16[192,32,16]{0,2,1:T(8,128)(2,1)}), bf16[192,32,16]{0,2,1:T(8,128)(2,1)S(1)}, u32[]{:S(2)}, u32[]{:S(2)}) async-start(bf16[192,32,16]{0,2,1:T(8,128)(2,1)} %bitcast.72), calls=%async_computation.1 | async-start | bytes 524288 | tf_op jit(solution)/shard_map/all_to_all | solution.py:133
  89.9 119.5 %all-gather.3.cloned.1.call-start = ((), (), s32[]{:S(2)}) async-start(), calls=%async_computation.4 | async-start | bytes 7962624 | tf_op jit(solution)/shard_map/all_gather | solution.py:145
  102.7 186.8 %reduce-scatter.2.cloned.1.call-start = ((), (), s32[]{:S(2)}) async-start(), calls=%async_computation.3 | async-start | bytes 1966080 | tf_op jit(solution)/shard_map/reduce_scatter | solution.py:148
Sparse Core Ops, SparseCore 0:
  102.8 106.5 all-gather.2
  263.0 26.3 reduce-scatter.1
where the time goes:
time: 298 us; the launch traced here: 296 us
  waiting for transfers between devices  142 us (48%)
  other arithmetic  50.1 us (17%)
  matrix products  38.8 us (13%)
  local copies, waits for them, and re-layouts  38 us (13%)
  between operations  13.6 us (5%)
  starting transfers between devices  13.4 us (4%)
    all_gather x1, waiting for transfers between devices, per_device(): lax.all_gather(injection, 'line', axis=0, tiled=True)  107 us
    convert_element_type x1, other arithmetic, site_power(): return (site_capacity * plane / 1000.0).astype(jnp.bfloat16)  32.6 us
    dot_general x1, matrix products, per_device(): jnp.dot(transfer_factors, lax.all_gather(injection, 'line', axis=0, tiled...  31.1 us
    reduce_scatter x1, waiting for transfers between devices, per_device(): lax.psum_scatter(partial_flows, 'bus', scatter_dimension=1, tiled=True)  26.5 us
    unnamed x15, local copies, waits for them, and re-layouts  12.8 us
    all_gather x1, local copies, waits for them, and re-layouts, per_device(): lax.all_gather(injection, 'line', axis=0, tiled=True)  9.83 us
    all_to_all x1, waiting for transfers between devices, per_device(): lax.all_to_all(outgoing, ('line', 'bus'), split_axis=1, concat_axis=1, ti...  9.25 us
    add x1, other arithmetic, site_power(): 1.0 + cos_tilt  7.51 us
  transfers between devices with their start and end apart: 4, of which 3 were waited for; matrix products, arithmetic and copies ran while one was open for 23% of the time, Pallas kernels for 0%

commit v1 on v0

--- a/solution.py
+++ b/solution.py
@@ -1,8 +1,11 @@
+import functools
 import math
 
 import jax
 import jax.numpy as jnp
 from jax import lax
+from jax.experimental import pallas as pl
+from jax.experimental.pallas import tpu as pltpu
 from jax.sharding import PartitionSpec as P
 
 BUSES = 70144
@@ -85,7 +88,7 @@
     return (site_capacity * plane / 1000.0).astype(jnp.bfloat16)
 
 
-def per_device(
+def general_device(
     clearness,
     cos_zenith,
     sun_azimuth,
@@ -148,6 +151,597 @@
     return lax.psum_scatter(partial_flows, "bus", scatter_dimension=1, tiled=True)
 
 
+LANES = 128
+ACOS_POLY = (
+    1.5707963262615365,
+    -0.21460172591625612,
+    0.08904479608150453,
+    -0.0507408012983321,
+    0.033314914408815,
+    -0.02284457168134235,
+    0.014575916928409219,
+    -0.00744564558483129,
+    0.002518626106102872,
+    -0.00040427332732297214,
+)
+COS_POLY = tuple((-1.0) ** k / math.factorial(2 * k) for k in range(8))
+SIN_POLY = tuple((-1.0) ** k / math.factorial(2 * k + 1) for k in range(8))
+EMPTY = 4095
+
+
+def horner(x, poly):
+    total = jnp.full_like(x, poly[-1])
+    for coefficient in poly[-2::-1]:
+        total = total * x + coefficient
+    return total
+
+
+def reduce_pi(x):
+    turns = jnp.floor(x * (1.0 / math.pi) + 0.5)
+    rest = (x - turns * 3.140625) - turns * 0.0009676535897932
+    odd = turns - 2.0 * jnp.floor(turns * 0.5)
+    return rest, 1.0 - 2.0 * odd
+
+
+def cosine(x):
+    rest, sign = reduce_pi(x)
+    return sign * horner(rest * rest, COS_POLY)
+
+
+def sine(x):
+    rest, sign = reduce_pi(x)
+    return sign * rest * horner(rest * rest, SIN_POLY)
+
+
+def to_column(row, eye):
+    return jnp.sum(jnp.where(eye, row, 0.0), axis=1, keepdims=True)
+
+
+def place_kernel(bus_ref, slot_ref, tags_ref, *, owners, group_buses, cap, n_line, n_bus):
+    n_sites = bus_ref.shape[1]
+    bus = bus_ref[...]
+    group = jnp.zeros(bus.shape, jnp.int32)
+    for k in range(1, owners):
+        group = group + (bus >= k * group_buses).astype(jnp.int32)
+    local = (bus - group * group_buses).astype(jnp.float32)
+    group = group.astype(jnp.float32)
+    first = lax.broadcasted_iota(jnp.int32, (n_sites, n_sites), 0)
+    second = lax.broadcasted_iota(jnp.int32, (n_sites, n_sites), 1)
+    eye = first == second
+    earlier = (to_column(group, eye) == group) & (first < second)
+    position = jnp.sum(jnp.where(earlier, 1.0, 0.0), axis=0, keepdims=True)
+    slot = group * float(cap) + position
+    slot_ref[...] = slot.astype(jnp.int32)
+    slot_column = to_column(slot, eye).astype(jnp.int32)
+    local_column = to_column(local, eye)
+    n_slots = n_line * cap
+    for bus_index in range(n_bus):
+        lanes = lax.broadcasted_iota(jnp.int32, (n_sites, n_slots), 1) + bus_index * n_slots
+        hit = slot_column == lanes
+        tag = jnp.sum(jnp.where(hit, local_column + 1.0, 0.0), axis=0, keepdims=True)
+        tag = jnp.where(tag > 0.5, tag - 1.0, float(EMPTY)).astype(jnp.int32)
+        for line_index in range(n_line):
+            row = line_index * n_bus + bus_index
+            tags_ref[row : row + 1, :] = tag
+
+
+def place_sites(site_bus, owners, group_buses, cap, n_line, n_bus):
+    n_sites = site_bus.shape[0]
+    return pl.pallas_call(
+        functools.partial(
+            place_kernel,
+            owners=owners,
+            group_buses=group_buses,
+            cap=cap,
+            n_line=n_line,
+            n_bus=n_bus,
+        ),
+        out_shape=(
+            jax.ShapeDtypeStruct((1, n_sites), jnp.int32),
+            jax.ShapeDtypeStruct((owners, n_line * cap), jnp.int32),
+        ),
+        cost_estimate=pl.CostEstimate(flops=10**6, bytes_accessed=10**5, transcendentals=0),
+        name="place",
+    )(site_bus.reshape(1, n_sites))
+
+
+def power_kernel(
+    tilt_ref,
+    azimuth_ref,
+    clear_ref,
+    cosz_ref,
+    sun_ref,
+    cell_ref,
+    sky_ref,
+    dirint_ref,
+    perez_ref,
+    tilt_class_ref,
+    azimuth_class_ref,
+    capacity_ref,
+    slot_ref,
+    out_ref,
+    power_ref,
+    *,
+    n_line,
+    n_bus,
+    cap,
+    rows,
+):
+    n_hours, n_sites = clear_ref.shape
+    tilt_class = tilt_class_ref[...]
+    azimuth_class = azimuth_class_ref[...]
+    tilt = jnp.zeros(tilt_class.shape, jnp.float32)
+    for entry in range(TILTS):
+        tilt = jnp.where(tilt_class == entry, tilt_ref[entry], tilt)
+    azimuth = jnp.zeros(tilt_class.shape, jnp.float32)
+    for entry in range(AZIMS):
+        azimuth = jnp.where(azimuth_class == entry, azimuth_ref[entry], azimuth)
+    wide = (rows, LANES)
+    for part in range(n_sites // LANES):
+        lanes = slice(part * LANES, (part + 1) * LANES)
+        tilt_part = tilt[:, lanes]
+        cos_tilt = jnp.broadcast_to(cosine(tilt_part), wide)
+        sin_tilt = jnp.broadcast_to(sine(tilt_part), wide)
+        array_azimuth = jnp.broadcast_to(azimuth[:, lanes], wide)
+        site_capacity = jnp.broadcast_to(capacity_ref[:, lanes], wide)
+
+        def step(index, carry):
+            at = pl.ds(pl.multiple_of(index * rows, rows), rows)
+            clear = clear_ref[at, lanes]
+            cosz = cosz_ref[at, lanes]
+            sun_az = sun_ref[at, lanes]
+            cell = cell_ref[at, lanes]
+            sky = sky_ref[at, lanes]
+            global_flat = clear * solar_constant * cosz
+            zenith = jnp.sqrt(1.0 - cosz) * horner(cosz, ACOS_POLY)
+            sin_zenith = jnp.sqrt((1.0 - cosz) * (1.0 + cosz))
+            height = 96.07995 - zenith * (180.0 / math.pi)
+            airmass = 1.0 / (cosz + 0.50572 * jnp.exp(-1.6364 * jnp.log(height)))
+            clear_beam = horner(airmass, (0.866, -0.122, 0.0121, -0.000653, 1.4e-05))
+            part_a = horner(clear, (0.512, -1.56, 2.286, -2.222))
+            part_b = 0.37 + 0.962 * clear
+            part_c = horner(clear, (-0.28, 0.932, -2.048))
+            beam = jnp.maximum(clear_beam - (part_a + part_b * jnp.exp(part_c * airmass)), 0.0)
+            low = cell & (LANES - 1)
+            high = cell >> 7
+            coefficient = jnp.zeros(wide, jnp.float32)
+            for row in range(dirint_ref.shape[0]):
+                line = jnp.broadcast_to(dirint_ref[row : row + 1, :], wide)
+                found = jnp.take_along_axis(line, low, axis=1, mode="promise_in_bounds")
+                coefficient = jnp.where(high == row, found, coefficient)
+            direct = solar_constant * beam * coefficient
+            diffuse = jnp.maximum(global_flat - direct * cosz, 0.1 * global_flat)
+            bright = diffuse * airmass * (1.0 / solar_constant)
+            factor = [
+                jnp.take_along_axis(
+                    jnp.broadcast_to(perez_ref[row : row + 1, :], wide),
+                    sky,
+                    axis=1,
+                    mode="promise_in_bounds",
+                )
+                for row in range(6)
+            ]
+            circumsolar = jnp.maximum(0.0, factor[0] + factor[1] * bright + factor[2] * zenith)
+            horizon = factor[3] + factor[4] * bright + factor[5] * zenith
+            facing = jnp.maximum(
+                cosz * cos_tilt + sin_zenith * sin_tilt * cosine(sun_az - array_azimuth), 0.0
+            )
+            sky_part = diffuse * (
+                (1.0 - circumsolar) * (1.0 + cos_tilt) * 0.5
+                + circumsolar * facing / jnp.maximum(cosz, cos_limit)
+                + horizon * sin_tilt
+            )
+            plane = direct * facing + sky_part + albedo * global_flat * (1.0 - cos_tilt) * 0.5
+            power_ref[at, lanes] = (site_capacity * plane / 1000.0).astype(jnp.bfloat16)
+            return carry
+
+        lax.fori_loop(0, n_hours // rows, step, 0)
+
+    power = power_ref[...]
+    low_hours = power[:LANES]
+    rest = power[LANES:]
+    blank = jnp.zeros_like(rest)
+    left = jnp.concatenate([rest, blank], axis=0)
+    right = jnp.concatenate([blank, rest], axis=0)
+    slot = slot_ref[...]
+    n_slots = n_line * cap
+    half = cap // 2
+    dims = (((1,), (1,)), ((), ()))
+    for bus_index in range(n_bus):
+        base = bus_index * n_slots
+        slots = lax.broadcasted_iota(jnp.int32, (n_slots, n_sites), 0) + base
+        pick = jnp.where(slots == slot, 1.0, 0.0).astype(jnp.bfloat16)
+        top = lax.dot_general(pick, low_hours, dims, preferred_element_type=jnp.float32)
+        index = lax.broadcasted_iota(jnp.int32, (n_slots // 2, n_sites), 0)
+        paired = (index // half) * cap + index % half + base
+        pick_left = jnp.where(paired == slot, 1.0, 0.0).astype(jnp.bfloat16)
+        pick_right = jnp.where(paired + half == slot, 1.0, 0.0).astype(jnp.bfloat16)
+        bottom = lax.dot_general(
+            pick_left, left, dims, preferred_element_type=jnp.float32
+        ) + lax.dot_general(pick_right, right, dims, preferred_element_type=jnp.float32)
+        top = top.astype(jnp.bfloat16)
+        bottom = bottom.astype(jnp.bfloat16)
+        for line_index in range(n_line):
+            row = line_index * n_bus + bus_index
+            out_ref[row, :n_slots, :] = top
+            out_ref[row, n_slots:, :] = bottom
+
+
+def packed_power(
+    tilt_table,
+    azimuth_table,
+    hourly,
+    dirint_coef,
+    perez_coef,
+    tilt_class,
+    azimuth_class,
+    capacity,
+    slot,
+    n_line,
+    n_bus,
+    cap,
+):
+    n_hours, n_sites = hourly[0].shape
+    owners = n_line * n_bus
+    n_slots = n_line * cap
+    rows_of = -(-dirint_coef.shape[0] // LANES)
+    dirint = jnp.pad(dirint_coef, (0, rows_of * LANES - dirint_coef.shape[0]))
+    dirint = dirint.reshape(rows_of, LANES)
+    perez = jnp.pad(perez_coef, ((0, 2), (0, LANES - perez_coef.shape[1])))
+    smem = pl.BlockSpec(memory_space=pltpu.SMEM)
+    vmem = pl.BlockSpec(memory_space=pltpu.VMEM)
+    return pl.pallas_call(
+        functools.partial(power_kernel, n_line=n_line, n_bus=n_bus, cap=cap, rows=32),
+        out_shape=jax.ShapeDtypeStruct((owners, n_slots * n_hours // LANES, LANES), jnp.bfloat16),
+        in_specs=[smem, smem] + [vmem] * 11,
+        out_specs=vmem,
+        scratch_shapes=[pltpu.VMEM((n_hours, n_sites), jnp.bfloat16)],
+        compiler_params=pltpu.CompilerParams(vmem_limit_bytes=32 << 20),
+        cost_estimate=pl.CostEstimate(
+            flops=2 * 10**8, bytes_accessed=3 * 10**6, transcendentals=2 * 10**5
+        ),
+        name="power",
+    )(
+        tilt_table,
+        azimuth_table,
+        *hourly,
+        dirint,
+        perez,
+        tilt_class.reshape(1, n_sites),
+        azimuth_class.reshape(1, n_sites),
+        capacity.reshape(1, n_sites),
+        slot,
+    )
+
+
+def order_kernel(tags_ref, sorted_ref, rank_ref):
+    n_groups, n_slots = tags_ref.shape
+    tags = tags_ref[...].astype(jnp.float32)
+    columns = jnp.transpose(tags)
+    lanes = lax.broadcasted_iota(jnp.int32, (n_slots, n_slots), 1)
+    row_index = lax.broadcasted_iota(jnp.int32, (1, n_slots), 1).astype(jnp.float32)
+    column_index = lax.broadcasted_iota(jnp.int32, (n_slots, 1), 0).astype(jnp.float32)
+    for g in range(n_groups):
+        column = columns[:, g : g + 1]
+        key_row = tags[g : g + 1] * n_slots + row_index
+        key_column = column * n_slots + column_index
+        rank_row = jnp.sum(jnp.where(key_column < key_row, 1.0, 0.0), axis=0, keepdims=True)
+        rank_column = jnp.sum(jnp.where(key_row < key_column, 1.0, 0.0), axis=1, keepdims=True)
+        hit = rank_column.astype(jnp.int32) == lanes
+        ordered = jnp.sum(jnp.where(hit, column, 0.0), axis=0, keepdims=True)
+        sorted_ref[g : g + 1, :] = ordered.astype(jnp.int32)
+        rank_ref[g : g + 1, :] = rank_row.astype(jnp.int32)
+
+
+def order_slots(tags):
+    shape = jax.ShapeDtypeStruct(tags.shape, jnp.int32)
+    return pl.pallas_call(
+        order_kernel,
+        out_shape=(shape, shape),
+        compiler_params=pltpu.CompilerParams(vmem_limit_bytes=32 << 20),
+        cost_estimate=pl.CostEstimate(flops=10**7, bytes_accessed=10**5, transcendentals=0),
+        name="order",
+    )(tags)
+
+
+def select_kernel(
+    plan_ref, sorted_ref, factors_ref, out_ref, buffer, pick, sems, *, group_buses, window, seg
+):
+    g = pl.program_id(0)
+    n_groups = pl.num_programs(0)
+    n_slots = out_ref.shape[1]
+    half = n_slots // 2
+    n_seg = window // seg
+
+    def copy(index):
+        start = pl.multiple_of((index * group_buses) // LANES * LANES, LANES)
+        slot = lax.rem(index, 2)
+        return pltpu.make_async_copy(
+            factors_ref.at[:, pl.ds(start, window)], buffer.at[slot], sems.at[slot]
+        )
+
+    @pl.when(g == 0)
+    def _():
+        copy(g).start()
+
+    @pl.when(g + 1 < n_groups)
+    def _():
+        copy(g + 1).start()
+
+    offset = lax.rem(g * group_buses, LANES)
+    last_first = plan_ref[0, g]
+    first_second = plan_ref[1, g]
+    place = sorted_ref[pl.ds(g, 1), :] + offset
+
+    def wanted(chunk, k):
+        if chunk == 0:
+            return k <= last_first
+        return k >= first_second
+
+    for chunk in range(2):
+        columns = slice(chunk * half, (chunk + 1) * half)
+        for k in range(n_seg):
+
+            @pl.when(wanted(chunk, k))
+            def _():
+                buses = lax.broadcasted_iota(jnp.int32, (seg, half), 0) + k * seg
+                pick[k * seg : (k + 1) * seg, columns] = jnp.where(
+                    buses == place[:, columns], 1.0, 0.0
+                ).astype(jnp.bfloat16)
+
+    copy(g).wait()
+    now = lax.rem(g, 2)
+    for chunk in range(2):
+        columns = slice(chunk * half, (chunk + 1) * half)
+        for k in range(n_seg):
+
+            @pl.when(wanted(chunk, k))
+            def _():
+                found = jnp.dot(
+                    buffer[now, :, k * seg : (k + 1) * seg],
+                    pick[k * seg : (k + 1) * seg, columns],
+                    preferred_element_type=jnp.float32,
+                ).astype(jnp.bfloat16)
+                if chunk == 0:
+                    begins = k == 0
+                else:
+                    begins = k == first_second
+
+                @pl.when(begins)
+                def _():
+                    out_ref[:, columns] = found
+
+                @pl.when(jnp.logical_not(begins))
+                def _():
+                    out_ref[:, columns] += found
+
+    @pl.when(first_second >= n_seg)
+    def _():
+        out_ref[:, half:] = jnp.zeros((out_ref.shape[0], half), jnp.bfloat16)
+
+
+def select_columns(plan, ordered, factors, group_buses, window, seg):
+    n_groups, n_slots = ordered.shape
+    n_lines = factors.shape[0]
+    return pl.pallas_call(
+        functools.partial(select_kernel, group_buses=group_buses, window=window, seg=seg),
+        grid=(n_groups,),
+        in_specs=[
+            pl.BlockSpec(memory_space=pltpu.SMEM),
+            pl.BlockSpec((n_groups, n_slots), lambda g: (0, 0)),
+            pl.BlockSpec(memory_space=pl.ANY),
+        ],
+        out_specs=pl.BlockSpec((n_lines, n_slots), lambda g: (0, g)),
+        out_shape=jax.ShapeDtypeStruct((n_lines, n_groups * n_slots), jnp.bfloat16),
+        scratch_shapes=[
+            pltpu.VMEM((2, n_lines, window), jnp.bfloat16),
+            pltpu.VMEM((window, n_slots), jnp.bfloat16),
+            pltpu.SemaphoreType.DMA((2,)),
+        ],
+        compiler_params=pltpu.CompilerParams(vmem_limit_bytes=48 << 20),
+        cost_estimate=pl.CostEstimate(
+            flops=2 * n_lines * window * n_groups * n_slots,
+            bytes_accessed=2 * n_lines * window * n_groups,
+            transcendentals=0,
+        ),
+        name="select",
+    )(plan, ordered, factors)
+
+
+def combine_kernel(plan_ref, core_ref, rank_ref, top_ref, bottom_ref, picked_ref, keep_ref, send_ref, acc, *, n_seg, n_bus):
+    g = pl.program_id(0)
+    n_lines, n_slots = picked_ref.shape
+    half = n_slots // 2
+    top = top_ref[...].reshape(n_slots, LANES)
+    bottom = bottom_ref[...].astype(jnp.float32)
+    blocks, rows, _ = bottom.shape
+    turned = pltpu.roll(bottom.reshape(blocks * rows, LANES), LANES // 2, 1)
+    bottom = jnp.concatenate([bottom, turned.reshape(blocks, rows, LANES)], axis=1)
+    bottom = bottom.reshape(n_slots, LANES).astype(jnp.bfloat16)
+    power = jnp.concatenate([top, bottom], axis=1)
+    rank = rank_ref[pl.ds(g, 1), :]
+    places = lax.broadcasted_iota(jnp.int32, (n_slots, n_slots), 0)
+    move = jnp.where(places == rank, 1.0, 0.0).astype(jnp.bfloat16)
+    power = jnp.dot(move, power, preferred_element_type=jnp.float32).astype(jnp.bfloat16)
+    flow = jnp.dot(picked_ref[:, :half], power[:half], preferred_element_type=jnp.float32)
+
+    @pl.when(g == 0)
+    def _():
+        acc[...] = jnp.zeros_like(acc)
+
+    acc[:n_lines, :] += flow
+
+    @pl.when(plan_ref[1, g] < n_seg)
+    def _():
+        acc[:n_lines, :] += jnp.dot(
+            picked_ref[:, half:], power[half:], preferred_element_type=jnp.float32
+        )
+
+    @pl.when(g == pl.num_programs(0) - 1)
+    def _():
+        turned = jnp.transpose(acc[...])
+        rows_each = keep_ref.shape[1]
+        for x in range(n_bus // 2):
+            pieces = [
+                turned[(2 * x + c) * rows_each : (2 * x + c + 1) * rows_each] for c in range(2)
+            ]
+
+            @pl.when(core_ref[0] == 0)
+            def _():
+                keep_ref[x] = pieces[0]
+                send_ref[x] = pieces[1]
+
+            @pl.when(core_ref[0] == 1)
+            def _():
+                keep_ref[x] = pieces[1]
+                send_ref[x] = pieces[0]
+
+
+def combine(plan, core, rank, arrived, picked, n_bus, n_hours, n_seg, cap):
+    n_groups, n_slots = rank.shape
+    n_lines = picked.shape[0]
+    owners = arrived.shape[0]
+    padded = -(-n_lines // LANES) * LANES
+    part = jax.ShapeDtypeStruct((n_bus // 2, n_hours // n_bus, padded), jnp.float32)
+    smem = pl.BlockSpec(memory_space=pltpu.SMEM)
+    offset = n_groups * cap // (cap // 2)
+    whole = pl.BlockSpec(part.shape, lambda g: (0, 0, 0))
+    return pl.pallas_call(
+        functools.partial(combine_kernel, n_seg=n_seg, n_bus=n_bus),
+        grid=(n_groups,),
+        in_specs=[
+            smem,
+            smem,
+            pl.BlockSpec((n_groups, n_slots), lambda g: (0, 0)),
+            pl.BlockSpec((owners, cap, LANES), lambda g: (0, g, 0)),
+            pl.BlockSpec((owners, cap // 2, LANES), lambda g: (0, offset + g, 0)),
+            pl.BlockSpec((n_lines, n_slots), lambda g: (0, g)),
+        ],
+        out_specs=(whole, whole),
+        out_shape=(part, part),
+        scratch_shapes=[pltpu.VMEM((padded, 2 * LANES), jnp.float32)],
+        compiler_params=pltpu.CompilerParams(vmem_limit_bytes=48 << 20),
+        cost_estimate=pl.CostEstimate(
+            flops=2 * n_lines * n_groups * n_slots * 256,
+            bytes_accessed=2 * n_lines * n_groups * n_slots,
+            transcendentals=0,
+        ),
+        name="combine",
+    )(plan, core, rank, arrived, arrived, picked)
+
+
+def finish_kernel(own_ref, other_ref, out_ref):
+    total = own_ref[...] + other_ref[...].astype(jnp.float32)
+    rows = out_ref.shape[1]
+    blank = jnp.zeros((LANES - rows, total.shape[1]), jnp.float32)
+    turned = jnp.transpose(jnp.concatenate([total, blank], axis=0))
+    out_ref[...] = turned[: out_ref.shape[0], :rows]
+
+
+def finish(own, other, n_lines):
+    return pl.pallas_call(
+        finish_kernel,
+        out_shape=jax.ShapeDtypeStruct((n_lines, own.shape[0]), jnp.float32),
+        compiler_params=pltpu.CompilerParams(vmem_limit_bytes=32 << 20),
+        name="finish",
+    )(own, other)
+
+
+def fast_device(
+    clearness,
+    cos_zenith,
+    sun_azimuth,
+    dirint_cell,
+    sky_bin,
+    dirint_coef,
+    perez_coef,
+    tilt_class,
+    azimuth_class,
+    tilt_table,
+    azimuth_table,
+    capacity,
+    site_bus,
+    transfer_factors,
+):
+    n_line = lax.axis_size("line")
+    n_bus = lax.axis_size("bus")
+    owners = n_line * n_bus
+    n_hours, n_sites = clearness.shape
+    n_lines, n_columns = transfer_factors.shape
+    group_buses = BUSES // owners
+    cap = 2 * n_sites // owners
+    window = window_of(group_buses)
+    seg = window // 3
+    slot, tags = place_sites(site_bus, owners, group_buses, cap, n_line, n_bus)
+    tags = lax.all_to_all(tags, ("line", "bus"), split_axis=0, concat_axis=0, tiled=True)
+    outgoing = packed_power(
+        tilt_table,
+        azimuth_table,
+        (clearness, cos_zenith, sun_azimuth, dirint_cell, sky_bin),
+        dirint_coef,
+        perez_coef,
+        tilt_class,
+        azimuth_class,
+        capacity,
+        slot,
+        n_line,
+        n_bus,
+        cap,
+    )
+    arrived = lax.all_to_all(outgoing, ("line", "bus"), split_axis=0, concat_axis=0, tiled=True)
+    tags = tags.reshape(owners, n_line, cap).transpose(1, 0, 2).reshape(n_line, owners * cap)
+    ordered, rank = order_slots(tags)
+    half = owners * cap // 2
+    offset = (jnp.arange(n_line, dtype=jnp.int32) * group_buses) % LANES
+    before = jnp.minimum((ordered[:, half - 1] + offset) // seg, window // seg - 1)
+    after = jnp.minimum((ordered[:, half] + offset) // seg, window // seg)
+    after = jnp.where(ordered[:, half] == EMPTY, window // seg, after)
+    plan = jnp.stack([before, after])
+    picked = select_columns(plan, ordered, transfer_factors, group_buses, window, seg)
+    place = lax.axis_index("bus")
+    core = (place % 2).reshape(1)
+    keep, send = combine(plan, core, rank, arrived, picked, n_bus, n_hours, window // seg, cap)
+    other_core = [(i, i ^ 1) for i in range(n_bus)]
+    other_chip = [(i, i ^ 2) for i in range(n_bus)]
+    summed = keep + lax.ppermute(send, "bus", other_core)
+    near = place // 2 == 0
+    own = jnp.where(near, summed[0], summed[1])
+    away = jnp.where(near, summed[1], summed[0]).astype(jnp.bfloat16)
+    return finish(own, lax.ppermute(away, "bus", other_chip), n_lines)
+
+
+def window_of(group_buses):
+    step = math.gcd(group_buses, LANES)
+    most = LANES - step + group_buses
+    return -(-most // LANES) * LANES
+
+
+def per_device(*arrays):
+    n_line = lax.axis_size("line")
+    n_bus = lax.axis_size("bus")
+    owners = n_line * n_bus
+    n_hours, n_sites = arrays[0].shape
+    n_lines, n_columns = arrays[-1].shape
+    group_buses = BUSES // owners
+    window = window_of(group_buses)
+    last = (n_line - 1) * group_buses // LANES * LANES
+    fits = (
+        n_bus == 4
+        and n_hours == 192
+        and n_sites == 2 * LANES
+        and n_sites * 2 == owners * 16
+        and n_line * 16 == LANES
+        and n_lines % 16 == 0
+        and n_columns % LANES == 0
+        and group_buses < EMPTY - LANES
+        and window % (3 * LANES) == 0
+        and last + window <= n_columns
+    )
+    if fits:
+        return fast_device(*arrays)
+    return general_device(*arrays)
+
+
 def solution(mesh):
     in_specs = (
         P(None, ("line", "bus")),

time: 298 us -> 99.3 us (0.33)
  waiting for transfers between devices: 142 us -> 9.14 us
  Pallas kernels: 0 us -> 64.6 us
  other arithmetic: 50.1 us -> 0.2 us
  matrix products: 38.8 us -> 0 us
  local copies, waits for them, and re-layouts: 38 us -> 11.6 us
  between operations: 13.6 us -> 0.14 us
    all_gather x1 -> x0, waiting for transfers between devices: 107 us -> none  [per_device(): lax.all_gather(injection, 'line', axis=0, tiled=True)]
    pallas_call x0 -> x6, Pallas kernels: none -> 64.6 us  [the longest x1 38.8 us: select_columns(): pl.pallas_call(functools.partial(select_kernel, group_buses=group_buses,...]
    dot_general x3 -> x0, matrix products: 38.8 us -> none  [the longest x1 31.1 us: per_device(): jnp.dot(transfer_factors, lax.all_gather(injection, 'line', axis=0, tiled...]
    convert_element_type x2 -> x1, other arithmetic: 32.6 us -> 0.04 us  [fast_device(): away = jnp.where(near, summed[1], summed[0]).astype(jnp.bfloat16)]
    reduce_scatter x1 -> x0, waiting for transfers between devices: 26.5 us -> none  [per_device(): lax.psum_scatter(partial_flows, 'bus', scatter_dimension=1, tiled=True)]
    all_gather x1 -> x0, local copies, waits for them, and re-layouts: 9.83 us -> none  [per_device(): lax.all_gather(injection, 'line', axis=0, tiled=True)]
    slice x6 -> x1, local copies, waits for them, and re-layouts: 9.53 us -> 0.18 us  [fast_device(): ordered[:, half - 1] + offset]
    all_to_all x2, waiting for transfers between devices: 9.25 us -> 0.01 us  [the longest x1 0.01 us: fast_device(): lax.all_to_all(tags, ('line', 'bus'), split_axis=0, concat_axis=0, tiled=...]
  transfers between devices with their start and end apart: 4 -> 4, of which waited for: 3 -> 2; matrix products, arithmetic and copies ran while one was open for 23% -> 2% of each run, Pallas kernels for 0% -> 48%
where the time goes in v1:
time: 99.3 us; the launch traced here: 98.9 us
  Pallas kernels  64.6 us (65%)
  starting transfers between devices  13.3 us (13%)
  local copies, waits for them, and re-layouts  11.6 us (12%)
  waiting for transfers between devices  9.14 us (9%)
    pallas_call x1, Pallas kernels, select_columns(): pl.pallas_call(functools.partial(select_kernel, group_buses=group_buses,...  38.8 us
    pallas_call x1, Pallas kernels, combine(): pl.pallas_call(functools.partial(combine_kernel, n_seg=n_seg, n_bus=n_bus...  15 us
    unnamed x22, local copies, waits for them, and re-layouts  8.65 us
    all_to_all x1, starting transfers between devices, fast_device(): lax.all_to_all(tags, ('line', 'bus'), split_axis=0, concat_axis=0, tiled=...  7.3 us
    ppermute x1, waiting for transfers between devices, fast_device(): return finish(own, lax.ppermute(away, 'bus', other_chip), n_lines)  6.88 us
    all_to_all x1, starting transfers between devices, fast_device(): lax.all_to_all(outgoing, ('line', 'bus'), split_axis=0, concat_axis=0, ti...  5.83 us
    pallas_call x1, Pallas kernels, packed_power(): pl.pallas_call(functools.partial(power_kernel, n_line=n_line, n_bus=n_bus...  5.15 us
    pallas_call x1, Pallas kernels, order_slots(): pl.pallas_call(order_kernel, out_shape=(shape, shape), compiler_params=pl...  3.64 us
  transfers between devices with their start and end apart: 4, of which 2 were waited for; matrix products, arithmetic and copies ran while one was open for 2% of the time, Pallas kernels for 48%

profile of v1, /device:TPU:0, one launch (start us, length us, event | category | flops | bytes accessed | tf_op | source)
XLA Modules:
  0.0 98.9 jit_solution(6238789667836479897)
XLA Ops:
  0.0 1.6 %place.1 = (s32[1,256]{1,0:T(1,128)}, s32[32,128]{1,0:T(8,128)}) custom-call(s32[1,256]{1,0:T(1,128)} %bitcast.33), custom_call_target="tpu_custom_call" | custom-call | flops 1000000 | bytes 100000 | tf_op jit(solution)/shard_map/place/pallas_call | solution.py:230
  1.6 7.3 %all-to-all-start = ((s32[32,1,128]{2,1,0:T(1,128)}), s32[32,1,128]{2,1,0:T(1,128)S(1)}, u32[]{:S(2)}, u32[]{:S(2)}) async-start(s32[32,1,128]{2,1,0:T(1,128)} %bitcast.32), calls=%async_computation | async-start | bytes 32768 | tf_op jit(solution)/shard_map/all_to_all | solution.py:676
  8.9 0.7 pad_bitcast_fusion.dirint_ref
  9.6 0.7 pad.9.perez_ref
  10.3 0.9 copy-done
  11.2 0.9 copy-done.1
  12.2 0.9 copy-done.2
  13.1 0.9 copy-done.3
  14.0 0.9 copy-done.4
  14.9 0.7 copy-done.5
  15.6 0.7 copy-done.6
  16.3 0.7 copy-done.7
  17.0 0.7 copy-done.8
  17.7 0.7 copy-done.9
  18.3 0.7 copy-done.10
  19.0 5.2 %power.1 = bf16[32,192,128]{2,1,0:T(8,128)(2,1)} custom-call(f32[8]{0:T(128)S(1)} %copy-done.9, f32[12]{0:T(128)S(1)} %copy-done.10, f32[192,256]{1,0:T(8,128)S(1)} %copy-done, f32[192,256]{1,0:T(8,128)S(1)} %copy-done.1, f32[192,256]{1,0:T(8,128)S(1)} %copy-done.2, s32[192,256]{1,0:T(8,128)S(1)} %copy-done.3, s32[192,256]{1,0:T(8,128)S(1)} %copy-done.4, ...), custom_call_target="tpu_custom_call" | custom-call | flops 200000000 | bytes 3000000 | tf_op jit(solution)/shard_map/power/pallas_call | solution.py:393
  24.1 5.8 %all-to-all-start.1 = ((bf16[32,192,128]{2,1,0:T(8,128)(2,1)}), bf16[32,192,128]{2,1,0:T(8,128)(2,1)S(1)}, u32[]{:S(2)}, u32[]{:S(2)}) async-start(bf16[32,192,128]{2,1,0:T(8,128)(2,1)} %power.1), calls=%async_computation.1 | async-start | bytes 3145728 | tf_op jit(solution)/shard_map/all_to_all | solution.py:691
  30.3 3.6 %order.1 = (s32[8,512]{1,0:T(8,128)S(1)}, s32[8,512]{1,0:T(8,128)S(1)}) custom-call(s32[8,512]{1,0:T(8,128)S(1)} %reshape.161.tags_ref), custom_call_target="tpu_custom_call" | custom-call | flops 10000000 | bytes 100000 | tf_op jit(solution)/shard_map/order/pallas_call | solution.py:438
  34.1 38.8 %select.29.picked_ref = bf16[2000,4096]{1,0:T(8,128)(2,1)} custom-call(s32[2,8]{1,0:T(2,128)S(1)} %pad_add_fusion.plan_ref, s32[8,512]{1,0:T(8,128)S(1)} %get-tuple-element.12.sorted_ref, bf16[2000,17536]{1,0:T(8,128)(2,1)} %factors_ref.1), custom_call_target="tpu_custom_call" | custom-call | flops 37748736000 | bytes 73728000 | tf_op jit(solution)/shard_map/select/pallas_call | solution.py:526
  73.0 15.0 %combine.1 = (f32[2,48,2048]{2,1,0:T(8,128)S(1)}, f32[2,48,2048]{2,1,0:T(8,128)S(1)}) custom-call(s32[2,8]{1,0:T(2,128)S(1)} %pad_add_fusion.plan_ref, s32[1]{0:T(128)} %bitcast.5.core_ref, s32[8,512]{1,0:T(8,128)S(1)} %get-tuple-element.13.rank_ref, bf16[32,192,128]{2,1,0:T(8,128)(2,1)S(1)} %all-to-all-done.1.top_ref.bottom_ref, ...), custom_call_target="tpu_custom_call" | custom-call | flops 4194304000 | bytes 16384000 | tf_op jit(solution)/shard_map/combine/pallas_call | solution.py:609
  88.1 2.3 %collective-permute-done = f32[2,48,2048]{2,1,0:T(8,128)S(1)} collective-permute-done((f32[2,48,2048]{2,1,0:T(8,128)S(1)}, f32[2,48,2048]{2,1,0:T(8,128)S(1)}, u32[]{:S(2)}, u32[]{:S(2)}) %collective-permute-start) | collective-permute-done | bytes 786464 | tf_op jit(solution)/shard_map/ppermute | solution.py:706
  90.6 6.9 %collective-permute-done.1.other_ref = bf16[48,2048]{1,0:T(8,128)(2,1)S(1)} collective-permute-done((bf16[48,2048]{1,0:T(8,128)(2,1)S(1)}, bf16[48,2048]{1,0:T(8,128)(2,1)S(1)}, u32[]{:S(2)}, u32[]{:S(2)}) %collective-permute-start.1) | collective-permute-done | bytes 196640 | tf_op jit(solution)/shard_map/ppermute | solution.py:710
  97.5 0.3 finish.1
  97.9 1.1 %copy.23 = f32[2000,48]{0,1:T(8,128)} copy(f32[2000,48]{1,0:T(8,128)S(1)} %finish.1) | data formatting | bytes 768000 | tf_op jit(solution)/shard_map/finish/pallas_call | solution.py:642
  (24 shorter events, 0.9 us)
Async XLA Ops:
  1.6 22.5 %all-to-all-start = ((s32[32,1,128]{2,1,0:T(1,128)}), s32[32,1,128]{2,1,0:T(1,128)S(1)}, u32[]{:S(2)}, u32[]{:S(2)}) async-start(s32[32,1,128]{2,1,0:T(1,128)} %bitcast.32), calls=%async_computation | async-start | bytes 32768 | tf_op jit(solution)/shard_map/all_to_all | solution.py:676
  10.3 0.9 copy-start
  11.2 0.9 copy-start.1
  12.2 0.9 copy-start.2
  13.1 0.9 copy-start.3
  14.0 0.9 copy-start.4
  14.9 0.7 copy-start.5
  15.6 0.7 copy-start.6
  16.3 0.7 copy-start.7
  17.0 0.7 copy-start.8
  17.6 0.7 copy-start.9
  18.3 0.7 copy-start.10
  24.1 48.9 %all-to-all-start.1 = ((bf16[32,192,128]{2,1,0:T(8,128)(2,1)}), bf16[32,192,128]{2,1,0:T(8,128)(2,1)S(1)}, u32[]{:S(2)}, u32[]{:S(2)}) async-start(bf16[32,192,128]{2,1,0:T(8,128)(2,1)} %power.1), calls=%async_computation.1 | async-start | bytes 3145728 | tf_op jit(solution)/shard_map/all_to_all | solution.py:691
  88.0 2.4 %collective-permute-start = (f32[2,48,2048]{2,1,0:T(8,128)S(1)}, f32[2,48,2048]{2,1,0:T(8,128)S(1)}, u32[]{:S(2)}, u32[]{:S(2)}) collective-permute-start(f32[2,48,2048]{2,1,0:T(8,128)S(1)} %get-tuple-element.16), channel_id=1, source_target_pairs={{0,1},{1,0},{2,3},{3,2},{4,5},{5,4},{6,7},{7,6},{8,9},{9,8},{10,11... | collective-permute-start | bytes 2359304 | tf_op jit(solution)/shard_map/ppermute | solution.py:706
  90.5 7.0 %collective-permute-start.1 = (bf16[48,2048]{1,0:T(8,128)(2,1)S(1)}, bf16[48,2048]{1,0:T(8,128)(2,1)S(1)}, u32[]{:S(2)}, u32[]{:S(2)}) collective-permute-start(bf16[48,2048]{1,0:T(8,128)(2,1)S(1)} %fusion), channel_id=1, source_target_pairs={{0,2},{1,3},{2,0},{3,1},{4,6},{5,7},{6,4},{7,5},{8,10},{9,11},{10,... | collective-permute-start | bytes 589832 | tf_op jit(solution)/shard_map/ppermute | solution.py:710

commit v2 on v1

--- a/solution.py
+++ b/solution.py
@@ -246,52 +246,60 @@
 
 
 def power_kernel(
-    tilt_ref,
-    azimuth_ref,
-    clear_ref,
-    cosz_ref,
-    sun_ref,
-    cell_ref,
-    sky_ref,
-    dirint_ref,
-    perez_ref,
-    tilt_class_ref,
-    azimuth_class_ref,
-    capacity_ref,
-    slot_ref,
-    out_ref,
-    power_ref,
-    *,
+    tilt_table_ref,
+    azimuth_table_ref,
+    *refs,
     n_line,
     n_bus,
     cap,
     rows,
 ):
-    n_hours, n_sites = clear_ref.shape
+    sources = refs[:11]
+    out_ref = refs[11]
+    held = refs[12:23]
+    power_ref, dirint_rows, perez_rows, sems = refs[23:]
+    copies = [
+        pltpu.make_async_copy(source, place, sems.at[i])
+        for i, (source, place) in enumerate(zip(sources, held))
+    ]
+    for copy in copies:
+        copy.start()
+    for copy in copies:
+        copy.wait()
+    clear_all, cosz_all, sun_all, cell_all, sky_all = held[:5]
+    dirint_ref, perez_ref, tilt_class_ref, azimuth_class_ref, capacity_ref, slot_ref = held[5:]
+    n_hours, n_sites = clear_all.shape
+    cells = dirint_ref.shape[1]
+    dirint_rows[...] = jnp.zeros_like(dirint_rows)
+    dirint_rows[:, :cells] = dirint_ref[...]
+    perez_rows[...] = jnp.zeros_like(perez_rows)
+    perez_rows[: perez_ref.shape[0], : perez_ref.shape[1]] = perez_ref[...]
     tilt_class = tilt_class_ref[...]
     azimuth_class = azimuth_class_ref[...]
     tilt = jnp.zeros(tilt_class.shape, jnp.float32)
     for entry in range(TILTS):
-        tilt = jnp.where(tilt_class == entry, tilt_ref[entry], tilt)
+        tilt = jnp.where(tilt_class == entry, tilt_table_ref[entry], tilt)
     azimuth = jnp.zeros(tilt_class.shape, jnp.float32)
     for entry in range(AZIMS):
-        azimuth = jnp.where(azimuth_class == entry, azimuth_ref[entry], azimuth)
+        azimuth = jnp.where(azimuth_class == entry, azimuth_table_ref[entry], azimuth)
     wide = (rows, LANES)
-    for part in range(n_sites // LANES):
-        lanes = slice(part * LANES, (part + 1) * LANES)
-        tilt_part = tilt[:, lanes]
-        cos_tilt = jnp.broadcast_to(cosine(tilt_part), wide)
-        sin_tilt = jnp.broadcast_to(sine(tilt_part), wide)
-        array_azimuth = jnp.broadcast_to(azimuth[:, lanes], wide)
-        site_capacity = jnp.broadcast_to(capacity_ref[:, lanes], wide)
-
-        def step(index, carry):
-            at = pl.ds(pl.multiple_of(index * rows, rows), rows)
-            clear = clear_ref[at, lanes]
-            cosz = cosz_ref[at, lanes]
-            sun_az = sun_ref[at, lanes]
-            cell = cell_ref[at, lanes]
-            sky = sky_ref[at, lanes]
+    cos_tilts = cosine(tilt)
+    sin_tilts = sine(tilt)
+    capacity = capacity_ref[...]
+
+    def some_hours(now, carry):
+        at = pl.ds(pl.multiple_of(now * rows, rows), rows)
+        for part in range(n_sites // LANES):
+            lanes = slice(part * LANES, (part + 1) * LANES)
+            cos_tilt = jnp.broadcast_to(cos_tilts[:, lanes], wide)
+            sin_tilt = jnp.broadcast_to(sin_tilts[:, lanes], wide)
+            array_azimuth = jnp.broadcast_to(azimuth[:, lanes], wide)
+            site_capacity = jnp.broadcast_to(capacity[:, lanes], wide)
+            clear = clear_all[at, lanes]
+            cosz = cosz_all[at, lanes]
+            sun_az = sun_all[at, lanes]
+            cell = cell_all[at, lanes]
+            sky = sky_all[at, lanes]
             global_flat = clear * solar_constant * cosz
             zenith = jnp.sqrt(1.0 - cosz) * horner(cosz, ACOS_POLY)
             sin_zenith = jnp.sqrt((1.0 - cosz) * (1.0 + cosz))
@@ -305,16 +313,18 @@
             low = cell & (LANES - 1)
             high = cell >> 7
             coefficient = jnp.zeros(wide, jnp.float32)
-            for row in range(dirint_ref.shape[0]):
-                line = jnp.broadcast_to(dirint_ref[row : row + 1, :], wide)
-                found = jnp.take_along_axis(line, low, axis=1, mode="promise_in_bounds")
+            for row in range(dirint_rows.shape[1] // LANES):
+                line = dirint_rows[:, row * LANES : (row + 1) * LANES]
+                found = jnp.take_along_axis(
+                    jnp.broadcast_to(line, wide), low, axis=1, mode="promise_in_bounds"
+                )
                 coefficient = jnp.where(high == row, found, coefficient)
             direct = solar_constant * beam * coefficient
             diffuse = jnp.maximum(global_flat - direct * cosz, 0.1 * global_flat)
             bright = diffuse * airmass * (1.0 / solar_constant)
             factor = [
                 jnp.take_along_axis(
-                    jnp.broadcast_to(perez_ref[row : row + 1, :], wide),
+                    jnp.broadcast_to(perez_rows[row : row + 1, :], wide),
                     sky,
                     axis=1,
                     mode="promise_in_bounds",
@@ -333,10 +343,9 @@
             )
             plane = direct * facing + sky_part + albedo * global_flat * (1.0 - cos_tilt) * 0.5
             power_ref[at, lanes] = (site_capacity * plane / 1000.0).astype(jnp.bfloat16)
-            return carry
-
-        lax.fori_loop(0, n_hours // rows, step, 0)
-
+        return carry
+
+    lax.fori_loop(0, n_hours // rows, some_hours, 0)
     power = power_ref[...]
     low_hours = power[:LANES]
     rest = power[LANES:]
@@ -384,68 +393,84 @@
     n_hours, n_sites = hourly[0].shape
     owners = n_line * n_bus
     n_slots = n_line * cap
-    rows_of = -(-dirint_coef.shape[0] // LANES)
-    dirint = jnp.pad(dirint_coef, (0, rows_of * LANES - dirint_coef.shape[0]))
-    dirint = dirint.reshape(rows_of, LANES)
-    perez = jnp.pad(perez_coef, ((0, 2), (0, LANES - perez_coef.shape[1])))
+    cells = dirint_coef.shape[0]
+    rows = 32
     smem = pl.BlockSpec(memory_space=pltpu.SMEM)
-    vmem = pl.BlockSpec(memory_space=pltpu.VMEM)
+    shape = (owners, n_slots * n_hours // LANES, LANES)
+    operands = (
+        *hourly,
+        dirint_coef.reshape(1, cells),
+        perez_coef,
+        tilt_class.reshape(1, n_sites),
+        azimuth_class.reshape(1, n_sites),
+        capacity.reshape(1, n_sites),
+        slot,
+    )
     return pl.pallas_call(
-        functools.partial(power_kernel, n_line=n_line, n_bus=n_bus, cap=cap, rows=32),
-        out_shape=jax.ShapeDtypeStruct((owners, n_slots * n_hours // LANES, LANES), jnp.bfloat16),
-        in_specs=[smem, smem] + [vmem] * 11,
-        out_specs=vmem,
-        scratch_shapes=[pltpu.VMEM((n_hours, n_sites), jnp.bfloat16)],
-        compiler_params=pltpu.CompilerParams(vmem_limit_bytes=32 << 20),
+        functools.partial(power_kernel, n_line=n_line, n_bus=n_bus, cap=cap, rows=rows),
+        out_shape=jax.ShapeDtypeStruct(shape, jnp.bfloat16),
+        in_specs=[smem, smem] + [pl.BlockSpec(memory_space=pltpu.HBM)] * len(operands),
+        out_specs=pl.BlockSpec(memory_space=pltpu.VMEM),
+        scratch_shapes=[pltpu.VMEM(x.shape, x.dtype) for x in operands]
+        + [
+            pltpu.VMEM((n_hours, n_sites), jnp.bfloat16),
+            pltpu.VMEM((1, -(-cells // LANES) * LANES), jnp.float32),
+            pltpu.VMEM((8, LANES), jnp.float32),
+            pltpu.SemaphoreType.DMA((len(operands),)),
+        ],
+        compiler_params=pltpu.CompilerParams(vmem_limit_bytes=64 << 20),
         cost_estimate=pl.CostEstimate(
             flops=2 * 10**8, bytes_accessed=3 * 10**6, transcendentals=2 * 10**5
         ),
         name="power",
-    )(
-        tilt_table,
-        azimuth_table,
-        *hourly,
-        dirint,
-        perez,
-        tilt_class.reshape(1, n_sites),
-        azimuth_class.reshape(1, n_sites),
-        capacity.reshape(1, n_sites),
-        slot,
-    )
-
-
-def order_kernel(tags_ref, sorted_ref, rank_ref):
+    )(tilt_table, azimuth_table, *operands)
+
+
+def order_slots(tags_ref, sorted_ref, rank_ref, plan_ref, group_buses):
     n_groups, n_slots = tags_ref.shape
+    half = n_slots // 2
     tags = tags_ref[...].astype(jnp.float32)
-    columns = jnp.transpose(tags)
-    lanes = lax.broadcasted_iota(jnp.int32, (n_slots, n_slots), 1)
-    row_index = lax.broadcasted_iota(jnp.int32, (1, n_slots), 1).astype(jnp.float32)
-    column_index = lax.broadcasted_iota(jnp.int32, (n_slots, 1), 0).astype(jnp.float32)
+    lanes = lax.broadcasted_iota(jnp.int32, (n_slots, n_slots), 1).astype(jnp.float32)
+    index = lax.broadcasted_iota(jnp.int32, (n_groups, n_slots), 1)
+    keys = tags * n_slots + index.astype(jnp.float32)
+    tag_columns = jnp.transpose(tags)
+    key_columns = jnp.transpose(keys)
+    ranks = []
     for g in range(n_groups):
-        column = columns[:, g : g + 1]
-        key_row = tags[g : g + 1] * n_slots + row_index
-        key_column = column * n_slots + column_index
-        rank_row = jnp.sum(jnp.where(key_column < key_row, 1.0, 0.0), axis=0, keepdims=True)
-        rank_column = jnp.sum(jnp.where(key_row < key_column, 1.0, 0.0), axis=1, keepdims=True)
-        hit = rank_column.astype(jnp.int32) == lanes
-        ordered = jnp.sum(jnp.where(hit, column, 0.0), axis=0, keepdims=True)
-        sorted_ref[g : g + 1, :] = ordered.astype(jnp.int32)
-        rank_ref[g : g + 1, :] = rank_row.astype(jnp.int32)
-
-
-def order_slots(tags):
-    shape = jax.ShapeDtypeStruct(tags.shape, jnp.int32)
-    return pl.pallas_call(
-        order_kernel,
-        out_shape=(shape, shape),
-        compiler_params=pltpu.CompilerParams(vmem_limit_bytes=32 << 20),
-        cost_estimate=pl.CostEstimate(flops=10**7, bytes_accessed=10**5, transcendentals=0),
-        name="order",
-    )(tags)
+        smaller = key_columns[:, g : g + 1] < keys[g : g + 1]
+        ranks.append(jnp.sum(jnp.where(smaller, 1.0, 0.0), axis=0, keepdims=True))
+    rank = jnp.concatenate(ranks, axis=0)
+    rank_ref[...] = rank.astype(jnp.int32)
+    rank_columns = jnp.transpose(rank)
+    ordered = []
+    for g in range(n_groups):
+        hit = rank_columns[:, g : g + 1] == lanes
+        found = jnp.sum(jnp.where(hit, tag_columns[:, g : g + 1], 0.0), axis=0, keepdims=True)
+        ordered.append(found + float(g * group_buses % LANES))
+    ordered = jnp.concatenate(ordered, axis=0)
+    sorted_ref[...] = ordered.astype(jnp.int32)
+    real = ordered < float(EMPTY)
+    last = jnp.max(jnp.where(real & (index < half), ordered, 0.0), axis=1, keepdims=True)
+    after = jnp.min(jnp.where(real & (index >= half), ordered, 2.0 * EMPTY), axis=1, keepdims=True)
+    for g in range(n_groups):
+        plan_ref[0, g] = jnp.max(last[g : g + 1]).astype(jnp.int32)
+        plan_ref[1, g] = jnp.max(after[g : g + 1]).astype(jnp.int32)
 
 
 def select_kernel(
-    plan_ref, sorted_ref, factors_ref, out_ref, buffer, pick, sems, *, group_buses, window, seg
+    tags_ref,
+    factors_ref,
+    out_ref,
+    rank_ref,
+    buffer,
+    pick,
+    sorted_ref,
+    plan_ref,
+    sems,
+    *,
+    group_buses,
+    window,
+    seg,
 ):
     g = pl.program_id(0)
     n_groups = pl.num_programs(0)
@@ -468,15 +493,18 @@
     def _():
         copy(g + 1).start()
 
-    offset = lax.rem(g * group_buses, LANES)
-    last_first = plan_ref[0, g]
-    first_second = plan_ref[1, g]
-    place = sorted_ref[pl.ds(g, 1), :] + offset
+    @pl.when(g == 0)
+    def _():
+        order_slots(tags_ref, sorted_ref, rank_ref, plan_ref, group_buses)
+
+    last = plan_ref[0, g]
+    after = plan_ref[1, g]
+    place = sorted_ref[pl.ds(g, 1), :]
 
     def wanted(chunk, k):
         if chunk == 0:
-            return k <= last_first
-        return k >= first_second
+            return last >= k * seg
+        return after < (k + 1) * seg
 
     for chunk in range(2):
         columns = slice(chunk * half, (chunk + 1) * half)
@@ -491,51 +519,52 @@
 
     copy(g).wait()
     now = lax.rem(g, 2)
-    for chunk in range(2):
-        columns = slice(chunk * half, (chunk + 1) * half)
-        for k in range(n_seg):
-
-            @pl.when(wanted(chunk, k))
-            def _():
-                found = jnp.dot(
-                    buffer[now, :, k * seg : (k + 1) * seg],
-                    pick[k * seg : (k + 1) * seg, columns],
-                    preferred_element_type=jnp.float32,
-                ).astype(jnp.bfloat16)
-                if chunk == 0:
-                    begins = k == 0
-                else:
-                    begins = k == first_second
-
-                @pl.when(begins)
-                def _():
-                    out_ref[:, columns] = found
-
-                @pl.when(jnp.logical_not(begins))
-                def _():
-                    out_ref[:, columns] += found
-
-    @pl.when(first_second >= n_seg)
+    for k in range(n_seg):
+        stop = (k + 1) * seg
+        begin = k * seg
+        ends_here = last < stop if k + 1 < n_seg else last >= begin
+        if 0 < k < n_seg - 1:
+            ends_here = ends_here & (last >= begin)
+
+        @pl.when(ends_here)
+        def _():
+            out_ref[:, :half] = jnp.dot(
+                buffer[now, :, :stop], pick[:stop, :half], preferred_element_type=jnp.float32
+            ).astype(jnp.bfloat16)
+
+        starts_here = after < stop
+        if k:
+            starts_here = starts_here & (after >= begin)
+
+        @pl.when(starts_here)
+        def _():
+            out_ref[:, half:] = jnp.dot(
+                buffer[now, :, begin:], pick[begin:, half:], preferred_element_type=jnp.float32
+            ).astype(jnp.bfloat16)
+
+    @pl.when(after >= window)
     def _():
         out_ref[:, half:] = jnp.zeros((out_ref.shape[0], half), jnp.bfloat16)
 
 
-def select_columns(plan, ordered, factors, group_buses, window, seg):
-    n_groups, n_slots = ordered.shape
+def select_columns(tags, factors, group_buses, window, seg):
+    n_groups, n_slots = tags.shape
     n_lines = factors.shape[0]
+    whole = pl.BlockSpec((n_groups, n_slots), lambda g: (0, 0))
     return pl.pallas_call(
         functools.partial(select_kernel, group_buses=group_buses, window=window, seg=seg),
         grid=(n_groups,),
-        in_specs=[
-            pl.BlockSpec(memory_space=pltpu.SMEM),
-            pl.BlockSpec((n_groups, n_slots), lambda g: (0, 0)),
-            pl.BlockSpec(memory_space=pl.ANY),
-        ],
-        out_specs=pl.BlockSpec((n_lines, n_slots), lambda g: (0, g)),
-        out_shape=jax.ShapeDtypeStruct((n_lines, n_groups * n_slots), jnp.bfloat16),
+        in_specs=[whole, pl.BlockSpec(memory_space=pltpu.HBM)],
+        out_specs=(pl.BlockSpec((n_lines, n_slots), lambda g: (0, g)), whole),
+        out_shape=(
+            jax.ShapeDtypeStruct((n_lines, n_groups * n_slots), jnp.bfloat16),
+            jax.ShapeDtypeStruct((n_groups, n_slots), jnp.int32),
+        ),
         scratch_shapes=[
             pltpu.VMEM((2, n_lines, window), jnp.bfloat16),
             pltpu.VMEM((window, n_slots), jnp.bfloat16),
+            pltpu.VMEM((n_groups, n_slots), jnp.int32),
+            pltpu.SMEM((2, n_groups), jnp.int32),
             pltpu.SemaphoreType.DMA((2,)),
         ],
         compiler_params=pltpu.CompilerParams(vmem_limit_bytes=48 << 20),
@@ -545,106 +574,124 @@
             transcendentals=0,
         ),
         name="select",
-    )(plan, ordered, factors)
-
-
-def combine_kernel(plan_ref, core_ref, rank_ref, top_ref, bottom_ref, picked_ref, keep_ref, send_ref, acc, *, n_seg, n_bus):
-    g = pl.program_id(0)
-    n_lines, n_slots = picked_ref.shape
-    half = n_slots // 2
-    top = top_ref[...].reshape(n_slots, LANES)
-    bottom = bottom_ref[...].astype(jnp.float32)
-    blocks, rows, _ = bottom.shape
-    turned = pltpu.roll(bottom.reshape(blocks * rows, LANES), LANES // 2, 1)
-    bottom = jnp.concatenate([bottom, turned.reshape(blocks, rows, LANES)], axis=1)
-    bottom = bottom.reshape(n_slots, LANES).astype(jnp.bfloat16)
-    power = jnp.concatenate([top, bottom], axis=1)
-    rank = rank_ref[pl.ds(g, 1), :]
+    )(tags, factors)
+
+
+def move_power(rank_ref, arrived_ref, moved_ref, cap):
+    n_groups, n_slots = rank_ref.shape
+    half = cap // 2
+    tops = n_groups * cap
     places = lax.broadcasted_iota(jnp.int32, (n_slots, n_slots), 0)
-    move = jnp.where(places == rank, 1.0, 0.0).astype(jnp.bfloat16)
-    power = jnp.dot(move, power, preferred_element_type=jnp.float32).astype(jnp.bfloat16)
-    flow = jnp.dot(picked_ref[:, :half], power[:half], preferred_element_type=jnp.float32)
-
-    @pl.when(g == 0)
+    for g in range(n_groups):
+        top = arrived_ref[:, g * cap : (g + 1) * cap, :].reshape(n_slots, LANES)
+        bottom = arrived_ref[:, tops + g * half : tops + (g + 1) * half, :].astype(jnp.float32)
+        blocks = bottom.shape[0]
+        turned = pltpu.roll(bottom.reshape(blocks * half, LANES), LANES // 2, 1)
+        bottom = jnp.concatenate([bottom, turned.reshape(blocks, half, LANES)], axis=1)
+        bottom = bottom.reshape(n_slots, LANES).astype(jnp.bfloat16)
+        power = jnp.concatenate([top, bottom], axis=1)
+        move = jnp.where(places == rank_ref[g : g + 1, :], 1.0, 0.0).astype(jnp.bfloat16)
+        moved = jnp.dot(move, power, preferred_element_type=jnp.float32)
+        moved_ref[g * n_slots : (g + 1) * n_slots, :] = moved.astype(jnp.bfloat16)
+
+
+def lines_kernel(
+    core_ref, rank_ref, arrived_ref, picked_ref, keep_a, send_a, keep_b, send_b, moved_ref, *, cap, first
+):
+    step = pl.program_id(0)
+
+    @pl.when(step == 0)
     def _():
-        acc[...] = jnp.zeros_like(acc)
-
-    acc[:n_lines, :] += flow
-
-    @pl.when(plan_ref[1, g] < n_seg)
+        move_power(rank_ref, arrived_ref, moved_ref, cap)
+
+    flow = jnp.dot(picked_ref[...], moved_ref[...], preferred_element_type=jnp.float32)
+    turned = jnp.transpose(flow)
+    rows_each = keep_a.shape[1]
+    core_zero = core_ref[0] == 0
+    keep = []
+    send = []
+    for x in range(keep_a.shape[0]):
+        begin = 2 * x * rows_each
+        even = turned[begin : begin + rows_each]
+        odd = turned[begin + rows_each : begin + 2 * rows_each]
+        keep.append(jnp.where(core_zero, even, odd))
+        send.append(jnp.where(core_zero, odd, even))
+
+    def write(keep_ref, send_ref):
+        for x in range(keep_ref.shape[0]):
+            keep_ref[x] = keep[x]
+            send_ref[x] = send[x]
+
+    @pl.when(step < first)
     def _():
-        acc[:n_lines, :] += jnp.dot(
-            picked_ref[:, half:], power[half:], preferred_element_type=jnp.float32
-        )
-
-    @pl.when(g == pl.num_programs(0) - 1)
+        write(keep_a, send_a)
+
+    @pl.when(step >= first)
     def _():
-        turned = jnp.transpose(acc[...])
-        rows_each = keep_ref.shape[1]
-        for x in range(n_bus // 2):
-            pieces = [
-                turned[(2 * x + c) * rows_each : (2 * x + c + 1) * rows_each] for c in range(2)
-            ]
-
-            @pl.when(core_ref[0] == 0)
-            def _():
-                keep_ref[x] = pieces[0]
-                send_ref[x] = pieces[1]
-
-            @pl.when(core_ref[0] == 1)
-            def _():
-                keep_ref[x] = pieces[1]
-                send_ref[x] = pieces[0]
-
-
-def combine(plan, core, rank, arrived, picked, n_bus, n_hours, n_seg, cap):
+        write(keep_b, send_b)
+
+
+def lines(core, rank, arrived, picked, n_bus, n_hours, cap, block):
     n_groups, n_slots = rank.shape
     n_lines = picked.shape[0]
-    owners = arrived.shape[0]
-    padded = -(-n_lines // LANES) * LANES
-    part = jax.ShapeDtypeStruct((n_bus // 2, n_hours // n_bus, padded), jnp.float32)
-    smem = pl.BlockSpec(memory_space=pltpu.SMEM)
-    offset = n_groups * cap // (cap // 2)
-    whole = pl.BlockSpec(part.shape, lambda g: (0, 0, 0))
+    steps = -(-n_lines // block)
+    first = -(-steps // 2)
+    shape = (n_bus // 2, n_hours // n_bus)
+
+    def early(i):
+        return (0, 0, jnp.minimum(i, first - 1))
+
+    def late(i):
+        return (0, 0, jnp.maximum(i - first, 0))
+
+    blocks = [pl.BlockSpec(shape + (block,), early)] * 2 + [pl.BlockSpec(shape + (block,), late)] * 2
+    counts = [first * block] * 2 + [(steps - first) * block] * 2
     return pl.pallas_call(
-        functools.partial(combine_kernel, n_seg=n_seg, n_bus=n_bus),
-        grid=(n_groups,),
+        functools.partial(lines_kernel, cap=cap, first=first),
+        grid=(steps,),
         in_specs=[
-            smem,
-            smem,
-            pl.BlockSpec((n_groups, n_slots), lambda g: (0, 0)),
-            pl.BlockSpec((owners, cap, LANES), lambda g: (0, g, 0)),
-            pl.BlockSpec((owners, cap // 2, LANES), lambda g: (0, offset + g, 0)),
-            pl.BlockSpec((n_lines, n_slots), lambda g: (0, g)),
+            pl.BlockSpec(memory_space=pltpu.SMEM),
+            pl.BlockSpec(rank.shape, lambda i: (0, 0)),
+            pl.BlockSpec(arrived.shape, lambda i: (0, 0, 0)),
+            pl.BlockSpec((block, picked.shape[1]), lambda i: (i, 0)),
         ],
-        out_specs=(whole, whole),
-        out_shape=(part, part),
-        scratch_shapes=[pltpu.VMEM((padded, 2 * LANES), jnp.float32)],
-        compiler_params=pltpu.CompilerParams(vmem_limit_bytes=48 << 20),
+        out_specs=blocks,
+        out_shape=[jax.ShapeDtypeStruct(shape + (count,), jnp.float32) for count in counts],
+        scratch_shapes=[pltpu.VMEM((n_groups * n_slots, 2 * LANES), jnp.bfloat16)],
+        compiler_params=pltpu.CompilerParams(vmem_limit_bytes=40 << 20),
         cost_estimate=pl.CostEstimate(
-            flops=2 * n_lines * n_groups * n_slots * 256,
+            flops=4 * n_lines * n_groups * n_slots * LANES,
             bytes_accessed=2 * n_lines * n_groups * n_slots,
             transcendentals=0,
         ),
-        name="combine",
-    )(plan, core, rank, arrived, arrived, picked)
-
-
-def finish_kernel(own_ref, other_ref, out_ref):
-    total = own_ref[...] + other_ref[...].astype(jnp.float32)
-    rows = out_ref.shape[1]
-    blank = jnp.zeros((LANES - rows, total.shape[1]), jnp.float32)
-    turned = jnp.transpose(jnp.concatenate([total, blank], axis=0))
-    out_ref[...] = turned[: out_ref.shape[0], :rows]
-
-
-def finish(own, other, n_lines):
+        name="lines",
+    )(core, rank, arrived, picked)
+
+
+def finish_kernel(*refs):
+    out_ref = refs[-1]
+    parts = refs[:-1]
+    begin = 0
+    for i in range(len(parts) // 2):
+        total = parts[2 * i][...] + parts[2 * i + 1][...].astype(jnp.float32)
+        count = min(total.shape[1], out_ref.shape[1] - begin)
+        out_ref[:, begin : begin + count] = total[:, :count]
+        begin += count
+
+
+def finish(parts, n_lines):
+    rows = parts[0].shape[0]
     return pl.pallas_call(
         finish_kernel,
-        out_shape=jax.ShapeDtypeStruct((n_lines, own.shape[0]), jnp.float32),
-        compiler_params=pltpu.CompilerParams(vmem_limit_bytes=32 << 20),
+        in_specs=[pl.BlockSpec(memory_space=pltpu.VMEM)] * len(parts),
+        out_specs=pl.BlockSpec(memory_space=pltpu.VMEM),
+        out_shape=jax.ShapeDtypeStruct((rows, n_lines), jnp.float32),
+        compiler_params=pltpu.CompilerParams(vmem_limit_bytes=64 << 20),
+        cost_estimate=pl.CostEstimate(
+            flops=n_lines * rows, bytes_accessed=12 * n_lines * rows, transcendentals=0
+        ),
         name="finish",
-    )(own, other)
+    )(*parts)
 
 
 def fast_device(
@@ -690,24 +737,23 @@
     )
     arrived = lax.all_to_all(outgoing, ("line", "bus"), split_axis=0, concat_axis=0, tiled=True)
     tags = tags.reshape(owners, n_line, cap).transpose(1, 0, 2).reshape(n_line, owners * cap)
-    ordered, rank = order_slots(tags)
-    half = owners * cap // 2
-    offset = (jnp.arange(n_line, dtype=jnp.int32) * group_buses) % LANES
-    before = jnp.minimum((ordered[:, half - 1] + offset) // seg, window // seg - 1)
-    after = jnp.minimum((ordered[:, half] + offset) // seg, window // seg)
-    after = jnp.where(ordered[:, half] == EMPTY, window // seg, after)
-    plan = jnp.stack([before, after])
-    picked = select_columns(plan, ordered, transfer_factors, group_buses, window, seg)
+    picked, rank = select_columns(tags, transfer_factors, group_buses, window, seg)
     place = lax.axis_index("bus")
     core = (place % 2).reshape(1)
-    keep, send = combine(plan, core, rank, arrived, picked, n_bus, n_hours, window // seg, cap)
+    near = place // 2 == 0
     other_core = [(i, i ^ 1) for i in range(n_bus)]
     other_chip = [(i, i ^ 2) for i in range(n_bus)]
-    summed = keep + lax.ppermute(send, "bus", other_core)
-    near = place // 2 == 0
-    own = jnp.where(near, summed[0], summed[1])
-    away = jnp.where(near, summed[1], summed[0]).astype(jnp.bfloat16)
-    return finish(own, lax.ppermute(away, "bus", other_chip), n_lines)
+    keep_a, send_a, keep_b, send_b = lines(
+        core, rank, arrived, picked, n_bus, n_hours, cap, 512
+    )
+    ends = []
+    for keep, send in ((keep_a, send_a), (keep_b, send_b)):
+        summed = keep + lax.ppermute(send, "bus", other_core)
+        own = jnp.where(near, summed[0], summed[1])
+        away = jnp.where(near, summed[1], summed[0]).astype(jnp.bfloat16)
+        away = lax.ppermute(away, "bus", other_chip)
+        ends += [own, away]
+    return finish(ends, n_lines).T
 
 
 def window_of(group_buses):

time: 99.3 us -> 82 us (0.83)
  Pallas kernels: 64.6 us -> 54.9 us
  local copies, waits for them, and re-layouts: 11.6 us -> 2.94 us
  waiting for transfers between devices: 9.14 us -> 6.11 us
  starting transfers between devices: 13.3 us -> 15.9 us
  other arithmetic: 0.2 us -> 1.52 us
    unnamed x22 -> x2, local copies, waits for them, and re-layouts: 8.65 us -> 0.64 us
    pallas_call x3 -> x2, Pallas kernels: 19 us -> 11.9 us  [the longest x1 10 us: lines(): pl.pallas_call(functools.partial(lines_kernel, cap=cap, first=first), gri...]
    pallas_call x1, Pallas kernels: 38.8 us -> 35.2 us  [select_columns(): pl.pallas_call(functools.partial(select_kernel, group_buses=group_buses,...]
    ppermute x1 -> x2, waiting for transfers between devices: 6.88 us -> 3.38 us  [fast_device(): away = lax.ppermute(away, 'bus', other_chip)]
    ppermute x1 -> x2, starting transfers between devices: 0.07 us -> 2.16 us  [fast_device(): away = lax.ppermute(away, 'bus', other_chip)]
    all_to_all x1, waiting for transfers between devices: 0.01 us -> 1.51 us  [fast_device(): lax.all_to_all(outgoing, ('line', 'bus'), split_axis=0, concat_axis=0, ti...]
    select_n x1 -> x2, other arithmetic: 0.04 us -> 1.39 us  [fast_device(): own = jnp.where(near, summed[0], summed[1])]
    pallas_call x1 -> x0, local copies, waits for them, and re-layouts: 1.07 us -> none  [finish(): pl.pallas_call(finish_kernel, out_shape=jax.ShapeDtypeStruct((n_lines, ow...]
  transfers between devices with their start and end apart: 4 -> 6, of which waited for: 2 -> 4; matrix products, arithmetic and copies ran while one was open for 2% -> 5% of each run, Pallas kernels for 48% -> 51%
where the time goes in v2:
time: 82 us; the launch traced here: 81.5 us
  Pallas kernels  54.9 us (67%)
  starting transfers between devices  15.9 us (19%)
  waiting for transfers between devices  6.11 us (7%)
  local copies, waits for them, and re-layouts  2.94 us (4%)
  other arithmetic  1.52 us (2%)
    pallas_call x1, Pallas kernels, select_columns(): pl.pallas_call(functools.partial(select_kernel, group_buses=group_buses,...  35.2 us
    pallas_call x1, Pallas kernels, lines(): pl.pallas_call(functools.partial(lines_kernel, cap=cap, first=first), gri...  10 us
    all_to_all x1, starting transfers between devices, fast_device(): lax.all_to_all(tags, ('line', 'bus'), split_axis=0, concat_axis=0, tiled=...  7.43 us
    pallas_call x1, Pallas kernels, packed_power(): pl.pallas_call(functools.partial(power_kernel, n_line=n_line, n_bus=n_bus...  6.18 us
    all_to_all x1, starting transfers between devices, fast_device(): lax.all_to_all(outgoing, ('line', 'bus'), split_axis=0, concat_axis=0, ti...  5.76 us
    ppermute x2, waiting for transfers between devices, fast_device(): away = lax.ppermute(away, 'bus', other_chip)  3.38 us
    ppermute x2, starting transfers between devices, fast_device(): away = lax.ppermute(away, 'bus', other_chip)  2.16 us
    pallas_call x1, Pallas kernels, finish(): pl.pallas_call(finish_kernel, in_specs=[pl.BlockSpec(memory_space=pltpu.V...  1.91 us
  transfers between devices with their start and end apart: 6, of which 4 were waited for; matrix products, arithmetic and copies ran while one was open for 5% of the time, Pallas kernels for 51%

profile of v2, /device:TPU:0, one launch (start us, length us, event | category | flops | bytes accessed | tf_op | source)
XLA Modules:
  0.0 81.5 jit_solution(8978753851210560775)
XLA Ops:
  0.0 1.6 %place.1 = (s32[1,256]{1,0:T(1,128)}, s32[32,128]{1,0:T(8,128)}) custom-call(s32[1,256]{1,0:T(1,128)} %bitcast.25), custom_call_target="tpu_custom_call" | custom-call | flops 1000000 | bytes 100000 | tf_op jit(solution)/shard_map/place/pallas_call | solution.py:230
  1.6 7.4 %all-to-all-start = ((s32[32,1,128]{2,1,0:T(1,128)}), s32[32,1,128]{2,1,0:T(1,128)}, u32[]{:S(2)}, u32[]{:S(2)}) async-start(s32[32,1,128]{2,1,0:T(1,128)} %bitcast.21), calls=%async_computation | async-start | bytes 32768 | tf_op jit(solution)/shard_map/all_to_all | solution.py:723
  9.0 1.3 %reshape.41.refs_5_ = f32[1,1260]{1,0:T(1,128)} reshape(f32[1260]{0:T(1024)} %param.19) | data formatting | bytes 10080 | tf_op jit(solution)/shard_map/reshape | solution.py:402
  10.3 6.2 %power.1 = bf16[32,192,128]{2,1,0:T(8,128)(2,1)} custom-call(f32[8]{0:T(128)} %tilt_table_ref.1, f32[12]{0:T(128)} %azimuth_table_ref.1, f32[192,256]{1,0:T(8,128)} %refs_0_.1, f32[192,256]{1,0:T(8,128)} %refs_1_.1, f32[192,256]{1,0:T(8,128)} %refs_2_.1, s32[192,256]{1,0:T(8,128)} %refs_3_.1, s32[192,256]{1,0:T(8,128)} %refs_4_.1, ...), custom_call_target="tpu_custom_call" | custom-call | flops 200000000 | bytes 3000000 | tf_op jit(solution)/shard_map/power/pallas_call | solution.py:409
  16.5 0.0 all-to-all-done
  16.5 5.8 %all-to-all-start.1 = ((bf16[32,192,128]{2,1,0:T(8,128)(2,1)}), bf16[32,192,128]{2,1,0:T(8,128)(2,1)S(1)}, u32[]{:S(2)}, u32[]{:S(2)}) async-start(bf16[32,192,128]{2,1,0:T(8,128)(2,1)} %power.1), calls=%async_computation.1 | async-start | bytes 3145728 | tf_op jit(solution)/shard_map/all_to_all | solution.py:738
  22.3 0.8 copy.19
  23.1 0.1 copy.20
  23.2 0.1 reshape.40.tags_ref
  23.3 35.2 %select.7 = (bf16[2000,4096]{1,0:T(8,128)(2,1)}, s32[8,512]{1,0:T(8,128)S(1)}) custom-call(s32[8,512]{1,0:T(8,128)S(1)} %reshape.40.tags_ref, bf16[2000,17536]{1,0:T(8,128)(2,1)} %factors_ref.1), custom_call_target="tpu_custom_call" | custom-call | flops 37748736000 | bytes 73728000 | tf_op jit(solution)/shard_map/select/pallas_call | solution.py:554
  58.5 1.5 %all-to-all-done.1.arrived_ref = bf16[32,192,128]{2,1,0:T(8,128)(2,1)S(1)} async-done(((bf16[32,192,128]{2,1,0:T(8,128)(2,1)}), bf16[32,192,128]{2,1,0:T(8,128)(2,1)S(1)}, u32[]{:S(2)}, u32[]{:S(2)}) %all-to-all-start.1) | async-done | bytes 1572896 | tf_op jit(solution)/shard_map/all_to_all | solution.py:738
  60.0 10.0 %lines.1 = (f32[2,48,1024]{2,1,0:T(8,128)S(1)}, f32[2,48,1024]{2,1,0:T(8,128)S(1)}, f32[2,48,1024]{2,1,0:T(8,128)S(1)}, f32[2,48,1024]{2,1,0:T(8,128)S(1)}) custom-call(s32[1]{0:T(128)} %bitcast.core_ref, s32[8,512]{1,0:T(8,128)S(1)} %get-tuple-element.14.rank_ref, bf16[32,192,128]{2,1,0:T(8,128)(2,1)S(1)} %all-to-all-done.1.arrived_ref, ...), custom_call_target="tpu_custom_call" | custom-call | flops 4194304000 | bytes 16384000 | tf_op jit(solution)/shard_map/lines/pallas_call | solution.py:649
  70.1 0.1 collective-permute-start
  70.2 0.5 collective-permute-start.2
  70.6 1.2 %collective-permute-done = f32[2,48,1024]{2,1,0:T(8,128)S(1)} collective-permute-done((f32[2,48,1024]{2,1,0:T(8,128)S(1)}, f32[2,48,1024]{2,1,0:T(8,128)S(1)}, u32[]{:S(2)}, u32[]{:S(2)}) %collective-permute-start) | collective-permute-done | bytes 393248 | tf_op jit(solution)/shard_map/ppermute | solution.py:751
  71.9 1.9 %collective-permute-start.1 = (bf16[48,1024]{1,0:T(8,128)(2,1)S(1)}, bf16[48,1024]{1,0:T(8,128)(2,1)S(1)}, u32[]{:S(2)}, u32[]{:S(2)}) collective-permute-start(bf16[48,1024]{1,0:T(8,128)(2,1)S(1)} %fusion), channel_id=1, source_target_pairs={{0,2},{1,3},{2,0},{3,1},{4,6},{5,7},{6,4},{7,5},{8,10},{9,11},{10,... | collective-permute-start | bytes 294920 | tf_op jit(solution)/shard_map/ppermute | solution.py:754
  73.9 0.7 select_bitcast_fusion.1.refs_0_
  74.6 0.0 collective-permute-done.2
  74.6 0.2 collective-permute-start.3
  74.9 0.7 select_bitcast_fusion.refs_2_
  75.6 1.6 %collective-permute-done.1.refs_1_ = bf16[48,1024]{1,0:T(8,128)(2,1)S(1)} collective-permute-done((bf16[48,1024]{1,0:T(8,128)(2,1)S(1)}, bf16[48,1024]{1,0:T(8,128)(2,1)S(1)}, u32[]{:S(2)}, u32[]{:S(2)}) %collective-permute-start.1) | collective-permute-done | bytes 98336 | tf_op jit(solution)/shard_map/ppermute | solution.py:754
  77.2 0.6 copy-done
  77.8 1.8 %collective-permute-done.3.refs_3_ = bf16[48,1024]{1,0:T(8,128)(2,1)} collective-permute-done((bf16[48,1024]{1,0:T(8,128)(2,1)S(1)}, bf16[48,1024]{1,0:T(8,128)(2,1)}, u32[]{:S(2)}, u32[]{:S(2)}) %collective-permute-start.3) | collective-permute-done | bytes 98336 | tf_op jit(solution)/shard_map/ppermute | solution.py:754
  79.6 1.9 %finish.1 = f32[48,2000]{1,0:T(8,128)} custom-call(f32[48,1024]{1,0:T(8,128)} %select_bitcast_fusion.1.refs_0_, bf16[48,1024]{1,0:T(8,128)(2,1)} %copy-done, f32[48,1024]{1,0:T(8,128)} %select_bitcast_fusion.refs_2_, bf16[48,1024]{1,0:T(8,128)(2,1)} %collective-permute-done.3.refs_3_), custom_call_target="tpu_custom_call" | custom-call | flops 96000 | bytes 1152000 | tf_op jit(solution)/shard_map/finish/pallas_call | solution.py:684
  (5 shorter events, 0.1 us)
Async XLA Ops:
  1.6 14.9 %all-to-all-start = ((s32[32,1,128]{2,1,0:T(1,128)}), s32[32,1,128]{2,1,0:T(1,128)}, u32[]{:S(2)}, u32[]{:S(2)}) async-start(s32[32,1,128]{2,1,0:T(1,128)} %bitcast.21), calls=%async_computation | async-start | bytes 32768 | tf_op jit(solution)/shard_map/all_to_all | solution.py:723
  16.5 43.5 %all-to-all-start.1 = ((bf16[32,192,128]{2,1,0:T(8,128)(2,1)}), bf16[32,192,128]{2,1,0:T(8,128)(2,1)S(1)}, u32[]{:S(2)}, u32[]{:S(2)}) async-start(bf16[32,192,128]{2,1,0:T(8,128)(2,1)} %power.1), calls=%async_computation.1 | async-start | bytes 3145728 | tf_op jit(solution)/shard_map/all_to_all | solution.py:738
  70.1 1.8 %collective-permute-start = (f32[2,48,1024]{2,1,0:T(8,128)S(1)}, f32[2,48,1024]{2,1,0:T(8,128)S(1)}, u32[]{:S(2)}, u32[]{:S(2)}) collective-permute-start(f32[2,48,1024]{2,1,0:T(8,128)S(1)} %get-tuple-element.18), channel_id=1, source_target_pairs={{0,1},{1,0},{2,3},{3,2},{4,5},{5,4},{6,7},{7,6},{8,9},{9,8},{10,11... | collective-permute-start | bytes 1179656 | tf_op jit(solution)/shard_map/ppermute | solution.py:751
  70.2 4.4 %collective-permute-start.2 = (f32[2,48,1024]{2,1,0:T(8,128)S(1)}, f32[2,48,1024]{2,1,0:T(8,128)S(1)}, u32[]{:S(2)}, u32[]{:S(2)}) collective-permute-start(f32[2,48,1024]{2,1,0:T(8,128)S(1)} %get-tuple-element.20), channel_id=1, source_target_pairs={{0,1},{1,0},{2,3},{3,2},{4,5},{5,4},{6,7},{7,6},{8,9},{9,8},{10,11... | collective-permute-start | bytes 1179656 | tf_op jit(solution)/shard_map/ppermute | solution.py:751
  71.9 5.2 %collective-permute-start.1 = (bf16[48,1024]{1,0:T(8,128)(2,1)S(1)}, bf16[48,1024]{1,0:T(8,128)(2,1)S(1)}, u32[]{:S(2)}, u32[]{:S(2)}) collective-permute-start(bf16[48,1024]{1,0:T(8,128)(2,1)S(1)} %fusion), channel_id=1, source_target_pairs={{0,2},{1,3},{2,0},{3,1},{4,6},{5,7},{6,4},{7,5},{8,10},{9,11},{10,... | collective-permute-start | bytes 294920 | tf_op jit(solution)/shard_map/ppermute | solution.py:754
  74.6 5.0 %collective-permute-start.3 = (bf16[48,1024]{1,0:T(8,128)(2,1)S(1)}, bf16[48,1024]{1,0:T(8,128)(2,1)}, u32[]{:S(2)}, u32[]{:S(2)}) collective-permute-start(bf16[48,1024]{1,0:T(8,128)(2,1)S(1)} %fusion.1), channel_id=1, source_target_pairs={{0,2},{1,3},{2,0},{3,1},{4,6},{5,7},{6,4},{7,5},{8,10},{9,11},{10,... | collective-permute-start | bytes 294920 | tf_op jit(solution)/shard_map/ppermute | solution.py:754
  77.2 0.6 copy-start

commit v3 on v2

--- a/solution.py
+++ b/solution.py
@@ -269,9 +269,11 @@
     clear_all, cosz_all, sun_all, cell_all, sky_all = held[:5]
     dirint_ref, perez_ref, tilt_class_ref, azimuth_class_ref, capacity_ref, slot_ref = held[5:]
     n_hours, n_sites = clear_all.shape
-    cells = dirint_ref.shape[1]
+    cells = dirint_ref.shape[0]
     dirint_rows[...] = jnp.zeros_like(dirint_rows)
-    dirint_rows[:, :cells] = dirint_ref[...]
+    for begin in range(0, cells, LANES):
+        count = min(LANES, cells - begin)
+        dirint_rows[:, begin : begin + count] = dirint_ref[begin : begin + count].reshape(1, count)
     perez_rows[...] = jnp.zeros_like(perez_rows)
     perez_rows[: perez_ref.shape[0], : perez_ref.shape[1]] = perez_ref[...]
     tilt_class = tilt_class_ref[...]
@@ -399,7 +401,7 @@
     shape = (owners, n_slots * n_hours // LANES, LANES)
     operands = (
         *hourly,
-        dirint_coef.reshape(1, cells),
+        dirint_coef,
         perez_coef,
         tilt_class.reshape(1, n_sites),
         azimuth_class.reshape(1, n_sites),
@@ -582,116 +584,115 @@
     half = cap // 2
     tops = n_groups * cap
     places = lax.broadcasted_iota(jnp.int32, (n_slots, n_slots), 0)
-    for g in range(n_groups):
-        top = arrived_ref[:, g * cap : (g + 1) * cap, :].reshape(n_slots, LANES)
-        bottom = arrived_ref[:, tops + g * half : tops + (g + 1) * half, :].astype(jnp.float32)
+
+    def one(g, carry):
+        top_at = pl.ds(pl.multiple_of(g * cap, cap), cap)
+        bottom_at = pl.ds(pl.multiple_of(tops + g * half, half), half)
+        top = arrived_ref[:, top_at, :].reshape(n_slots, LANES)
+        bottom = arrived_ref[:, bottom_at, :].astype(jnp.float32)
         blocks = bottom.shape[0]
         turned = pltpu.roll(bottom.reshape(blocks * half, LANES), LANES // 2, 1)
         bottom = jnp.concatenate([bottom, turned.reshape(blocks, half, LANES)], axis=1)
         bottom = bottom.reshape(n_slots, LANES).astype(jnp.bfloat16)
         power = jnp.concatenate([top, bottom], axis=1)
-        move = jnp.where(places == rank_ref[g : g + 1, :], 1.0, 0.0).astype(jnp.bfloat16)
+        move = jnp.where(places == rank_ref[pl.ds(g, 1), :], 1.0, 0.0).astype(jnp.bfloat16)
         moved = jnp.dot(move, power, preferred_element_type=jnp.float32)
-        moved_ref[g * n_slots : (g + 1) * n_slots, :] = moved.astype(jnp.bfloat16)
+        moved_ref[pl.ds(pl.multiple_of(g * n_slots, n_slots), n_slots), :] = moved.astype(
+            jnp.bfloat16
+        )
+        return carry
+
+    lax.fori_loop(0, n_groups, one, 0)
 
 
 def lines_kernel(
-    core_ref, rank_ref, arrived_ref, picked_ref, keep_a, send_a, keep_b, send_b, moved_ref, *, cap, first
+    core_ref, *refs, cap, begin, count, first
 ):
-    step = pl.program_id(0)
-
-    @pl.when(step == 0)
-    def _():
+    if first:
+        rank_ref, arrived_ref, picked_ref = refs[:3]
+        keep_ref, send_ref, moved_out, moved_ref, buffer, sems = refs[3:]
+    else:
+        moved_in, picked_ref = refs[:2]
+        keep_ref, send_ref, moved_ref, buffer, sems = refs[2:]
+    n_blocks = sems.shape[0] - 1
+    block = keep_ref.shape[2] // n_blocks
+    last_size = count - (n_blocks - 1) * block
+
+    def copy(i, size):
+        at = pl.multiple_of(i * block, 16)
+        return pltpu.make_async_copy(
+            picked_ref.at[pl.ds(begin + at, size)], buffer.at[pl.ds(at, size)], sems.at[i]
+        )
+
+    def each(act):
+        for i in range(n_blocks):
+            act(copy(i, block if i + 1 < n_blocks else last_size))
+
+    if first:
+        each(lambda c: c.start())
         move_power(rank_ref, arrived_ref, moved_ref, cap)
-
-    flow = jnp.dot(picked_ref[...], moved_ref[...], preferred_element_type=jnp.float32)
-    turned = jnp.transpose(flow)
-    rows_each = keep_a.shape[1]
+        out = pltpu.make_async_copy(moved_ref, moved_out, sems.at[n_blocks])
+        out.start()
+    else:
+        fetch = pltpu.make_async_copy(moved_in, moved_ref, sems.at[n_blocks])
+        fetch.start()
+        each(lambda c: c.start())
+        fetch.wait()
+    rows_each = keep_ref.shape[1]
     core_zero = core_ref[0] == 0
-    keep = []
-    send = []
-    for x in range(keep_a.shape[0]):
-        begin = 2 * x * rows_each
-        even = turned[begin : begin + rows_each]
-        odd = turned[begin + rows_each : begin + 2 * rows_each]
-        keep.append(jnp.where(core_zero, even, odd))
-        send.append(jnp.where(core_zero, odd, even))
-
-    def write(keep_ref, send_ref):
+
+    def one(i, carry):
+        @pl.when(i + 1 < n_blocks)
+        def _():
+            copy(i, block).wait()
+
+        @pl.when(i + 1 == n_blocks)
+        def _():
+            copy(i, last_size).wait()
+
+        at = pl.multiple_of(i * block, block)
+        flow = jnp.dot(
+            buffer[pl.ds(at, block), :], moved_ref[...], preferred_element_type=jnp.float32
+        )
+        turned = jnp.transpose(flow)
         for x in range(keep_ref.shape[0]):
-            keep_ref[x] = keep[x]
-            send_ref[x] = send[x]
-
-    @pl.when(step < first)
-    def _():
-        write(keep_a, send_a)
-
-    @pl.when(step >= first)
-    def _():
-        write(keep_b, send_b)
-
-
-def lines(core, rank, arrived, picked, n_bus, n_hours, cap, block):
-    n_groups, n_slots = rank.shape
-    n_lines = picked.shape[0]
-    steps = -(-n_lines // block)
-    first = -(-steps // 2)
-    shape = (n_bus // 2, n_hours // n_bus)
-
-    def early(i):
-        return (0, 0, jnp.minimum(i, first - 1))
-
-    def late(i):
-        return (0, 0, jnp.maximum(i - first, 0))
-
-    blocks = [pl.BlockSpec(shape + (block,), early)] * 2 + [pl.BlockSpec(shape + (block,), late)] * 2
-    counts = [first * block] * 2 + [(steps - first) * block] * 2
+            low = 2 * x * rows_each
+            even = turned[low : low + rows_each]
+            odd = turned[low + rows_each : low + 2 * rows_each]
+            keep_ref[x, :, pl.ds(at, block)] = jnp.where(core_zero, even, odd)
+            send_ref[x, :, pl.ds(at, block)] = jnp.where(core_zero, odd, even)
+        return carry
+
+    lax.fori_loop(0, n_blocks, one, 0)
+    if first:
+        out.wait()
+
+
+def lines(core, inputs, picked, shape, cap, begin, count, padded, moved_shape, first):
+    smem = pl.BlockSpec(memory_space=pltpu.SMEM)
+    vmem = pl.BlockSpec(memory_space=pltpu.VMEM)
+    hbm = pl.BlockSpec(memory_space=pltpu.HBM)
+    part = jax.ShapeDtypeStruct(shape + (padded,), jnp.float32)
+    moved = jax.ShapeDtypeStruct(moved_shape, jnp.bfloat16)
+    block = 512
     return pl.pallas_call(
-        functools.partial(lines_kernel, cap=cap, first=first),
-        grid=(steps,),
-        in_specs=[
-            pl.BlockSpec(memory_space=pltpu.SMEM),
-            pl.BlockSpec(rank.shape, lambda i: (0, 0)),
-            pl.BlockSpec(arrived.shape, lambda i: (0, 0, 0)),
-            pl.BlockSpec((block, picked.shape[1]), lambda i: (i, 0)),
+        functools.partial(lines_kernel, cap=cap, begin=begin, count=count, first=first),
+        in_specs=[smem] + ([vmem, vmem] if first else [hbm]) + [hbm],
+        out_specs=[vmem, vmem] + ([hbm] if first else []),
+        out_shape=[part, part] + ([moved] if first else []),
+        scratch_shapes=[
+            pltpu.VMEM(moved_shape, jnp.bfloat16),
+            pltpu.VMEM((padded, picked.shape[1]), jnp.bfloat16),
+            pltpu.SemaphoreType.DMA((padded // block + 1,)),
         ],
-        out_specs=blocks,
-        out_shape=[jax.ShapeDtypeStruct(shape + (count,), jnp.float32) for count in counts],
-        scratch_shapes=[pltpu.VMEM((n_groups * n_slots, 2 * LANES), jnp.bfloat16)],
-        compiler_params=pltpu.CompilerParams(vmem_limit_bytes=40 << 20),
+        compiler_params=pltpu.CompilerParams(vmem_limit_bytes=46 << 20),
         cost_estimate=pl.CostEstimate(
-            flops=4 * n_lines * n_groups * n_slots * LANES,
-            bytes_accessed=2 * n_lines * n_groups * n_slots,
+            flops=1 * 2 * count * moved_shape[0] * moved_shape[1],
+            bytes_accessed=1 * 2 * count * moved_shape[0],
             transcendentals=0,
         ),
-        name="lines",
-    )(core, rank, arrived, picked)
-
-
-def finish_kernel(*refs):
-    out_ref = refs[-1]
-    parts = refs[:-1]
-    begin = 0
-    for i in range(len(parts) // 2):
-        total = parts[2 * i][...] + parts[2 * i + 1][...].astype(jnp.float32)
-        count = min(total.shape[1], out_ref.shape[1] - begin)
-        out_ref[:, begin : begin + count] = total[:, :count]
-        begin += count
-
-
-def finish(parts, n_lines):
-    rows = parts[0].shape[0]
-    return pl.pallas_call(
-        finish_kernel,
-        in_specs=[pl.BlockSpec(memory_space=pltpu.VMEM)] * len(parts),
-        out_specs=pl.BlockSpec(memory_space=pltpu.VMEM),
-        out_shape=jax.ShapeDtypeStruct((rows, n_lines), jnp.float32),
-        compiler_params=pltpu.CompilerParams(vmem_limit_bytes=64 << 20),
-        cost_estimate=pl.CostEstimate(
-            flops=n_lines * rows, bytes_accessed=12 * n_lines * rows, transcendentals=0
-        ),
-        name="finish",
-    )(*parts)
+        name="first_lines" if first else "other_lines",
+    )(core, *inputs, picked)
 
 
 def fast_device(
@@ -743,8 +744,16 @@
     near = place // 2 == 0
     other_core = [(i, i ^ 1) for i in range(n_bus)]
     other_chip = [(i, i ^ 2) for i in range(n_bus)]
-    keep_a, send_a, keep_b, send_b = lines(
-        core, rank, arrived, picked, n_bus, n_hours, cap, 512
+    shape = (n_bus // 2, n_hours // n_bus)
+    moved_shape = (n_line * owners * cap, 2 * LANES)
+    half_lines = -(-n_lines // 1024) * 512
+    keep_a, send_a, moved = lines(
+        core, (rank, arrived), picked, shape, cap, 0, half_lines, half_lines, moved_shape, True
+    )
+    other = n_lines - half_lines
+    padded = -(-other // 512) * 512
+    keep_b, send_b = lines(
+        core, (moved,), picked, shape, cap, half_lines, other, padded, moved_shape, False
     )
     ends = []
     for keep, send in ((keep_a, send_a), (keep_b, send_b)):
@@ -752,8 +761,8 @@
         own = jnp.where(near, summed[0], summed[1])
         away = jnp.where(near, summed[1], summed[0]).astype(jnp.bfloat16)
         away = lax.ppermute(away, "bus", other_chip)
-        ends += [own, away]
-    return finish(ends, n_lines).T
+        ends.append(own + away.astype(jnp.float32))
+    return jnp.concatenate(ends, axis=1)[:, :n_lines].T
 
 
 def window_of(group_buses):

time: 82 us -> 78.7 us (0.960)
  local copies, waits for them, and re-layouts: 2.94 us -> 1.02 us
    pallas_call x1, Pallas kernels: 35.2 us -> 37 us  [select_columns(): pl.pallas_call(functools.partial(select_kernel, group_buses=group_buses,...]
    all_to_all x1, waiting for transfers between devices: 1.51 us -> 0.01 us  [fast_device(): lax.all_to_all(outgoing, ('line', 'bus'), split_axis=0, concat_axis=0, ti...]
    select_n x2 -> x0, other arithmetic: 1.39 us -> none  [fast_device(): own = jnp.where(near, summed[0], summed[1])]
    reshape x1 -> x0, local copies, waits for them, and re-layouts: 1.29 us -> none  [packed_power(): dirint_coef.reshape(1, cells)]
    ppermute x2, waiting for transfers between devices: 3.38 us -> 4.56 us  [fast_device(): away = lax.ppermute(away, 'bus', other_chip)]
    pallas_call x2, Pallas kernels: 11.9 us -> 10.9 us  [lines(): pl.pallas_call(functools.partial(lines_kernel, cap=cap, begin=begin, coun...]
    ppermute x2, waiting for transfers between devices: 1.21 us -> 0.31 us  [fast_device(): summed = keep + lax.ppermute(send, 'bus', other_core)]
  transfers between devices with their start and end apart: 6 -> 6, of which waited for: 4 -> 4; matrix products, arithmetic and copies ran while one was open for 5% -> 2% of each run, Pallas kernels for 51% -> 61%
where the time goes in v3:
time: 78.7 us; the launch traced here: 78.4 us
  Pallas kernels  55.6 us (71%)
  starting transfers between devices  15.1 us (19%)
  waiting for transfers between devices  5.58 us (7%)
  local copies, waits for them, and re-layouts  1.02 us (1%)
  other arithmetic  0.97 us (1%)
    pallas_call x1, Pallas kernels, select_columns(): pl.pallas_call(functools.partial(select_kernel, group_buses=group_buses,...  37 us
    pallas_call x2, Pallas kernels, lines(): pl.pallas_call(functools.partial(lines_kernel, cap=cap, begin=begin, coun...  10.9 us
    all_to_all x1, starting transfers between devices, fast_device(): lax.all_to_all(tags, ('line', 'bus'), split_axis=0, concat_axis=0, tiled=...  7.43 us
    pallas_call x1, Pallas kernels, packed_power(): pl.pallas_call(functools.partial(power_kernel, n_line=n_line, n_bus=n_bus...  6.18 us
    all_to_all x1, starting transfers between devices, fast_device(): lax.all_to_all(outgoing, ('line', 'bus'), split_axis=0, concat_axis=0, ti...  5.08 us
    ppermute x2, waiting for transfers between devices, fast_device(): away = lax.ppermute(away, 'bus', other_chip)  4.56 us
    ppermute x2, starting transfers between devices, fast_device(): away = lax.ppermute(away, 'bus', other_chip)  1.93 us
    pallas_call x1, Pallas kernels, place_sites(): pl.pallas_call(functools.partial(place_kernel, owners=owners, group_buses...  1.6 us
  transfers between devices with their start and end apart: 6, of which 4 were waited for; matrix products, arithmetic and copies ran while one was open for 2% of the time, Pallas kernels for 61%

profile of v3, /device:TPU:0, one launch (start us, length us, event | category | flops | bytes accessed | tf_op | source)
XLA Modules:
  0.0 78.4 jit_solution(16534624190244013776)
XLA Ops:
  0.0 1.6 %place.1 = (s32[1,256]{1,0:T(1,128)}, s32[32,128]{1,0:T(8,128)}) custom-call(s32[1,256]{1,0:T(1,128)} %bitcast.26), custom_call_target="tpu_custom_call" | custom-call | flops 1000000 | bytes 100000 | tf_op jit(solution)/shard_map/place/pallas_call | solution.py:230
  1.6 7.4 %all-to-all-start = ((s32[32,1,128]{2,1,0:T(1,128)}), s32[32,1,128]{2,1,0:T(1,128)}, u32[]{:S(2)}, u32[]{:S(2)}) async-start(s32[32,1,128]{2,1,0:T(1,128)} %bitcast.22), calls=%async_computation | async-start | bytes 32768 | tf_op jit(solution)/shard_map/all_to_all | solution.py:724
  9.0 6.2 %power.1 = bf16[32,192,128]{2,1,0:T(8,128)(2,1)} custom-call(f32[8]{0:T(128)} %tilt_table_ref.1, f32[12]{0:T(128)} %azimuth_table_ref.1, f32[192,256]{1,0:T(8,128)} %refs_0_.1, f32[192,256]{1,0:T(8,128)} %refs_1_.1, f32[192,256]{1,0:T(8,128)} %refs_2_.1, s32[192,256]{1,0:T(8,128)} %refs_3_.1, s32[192,256]{1,0:T(8,128)} %refs_4_.1, f32[1260]{0:T(1024)} %refs_5_.1, ...), custom_call_target="tpu_custom_call" | custom-call | flops 200000000 | bytes 3000000 | tf_op jit(solution)/shard_map/power/pallas_call | solution.py:411
  15.2 0.7 all-to-all-done
  15.9 5.1 %all-to-all-start.1 = ((bf16[32,192,128]{2,1,0:T(8,128)(2,1)}), bf16[32,192,128]{2,1,0:T(8,128)(2,1)S(1)}, u32[]{:S(2)}, u32[]{:S(2)}) async-start(bf16[32,192,128]{2,1,0:T(8,128)(2,1)} %power.1), calls=%async_computation.1 | async-start | bytes 3145728 | tf_op jit(solution)/shard_map/all_to_all | solution.py:739
  21.0 0.8 %copy.19 = s32[32,1,128]{0,2,1:T(8,128)S(1)} copy(s32[32,1,128]{2,1,0:T(1,128)} %all-to-all-done) | data formatting | bytes 32768 | tf_op jit(solution)/shard_map/all_to_all | solution.py:724
  21.8 0.1 copy.20
  21.9 0.1 reshape.37.tags_ref
  22.1 37.0 %select.7 = (bf16[2000,4096]{1,0:T(8,128)(2,1)}, s32[8,512]{1,0:T(8,128)S(1)}) custom-call(s32[8,512]{1,0:T(8,128)S(1)} %reshape.37.tags_ref, bf16[2000,17536]{1,0:T(8,128)(2,1)} %factors_ref.1), custom_call_target="tpu_custom_call" | custom-call | flops 37748736000 | bytes 73728000 | tf_op jit(solution)/shard_map/select/pallas_call | solution.py:556
  59.0 0.0 all-to-all-done.1.refs_1_
  59.0 5.9 %first_lines.1 = (f32[2,48,1024]{2,1,0:T(8,128)S(1)}, f32[2,48,1024]{2,1,0:T(8,128)S(1)}, bf16[4096,256]{1,0:T(8,128)(2,1)S(1)}) custom-call(s32[1]{0:T(128)} %bitcast.core_ref, s32[8,512]{1,0:T(8,128)S(1)} %get-tuple-element.15.refs_0_, bf16[32,192,128]{2,1,0:T(8,128)(2,1)S(1)} %all-to-all-done.1.refs_1_, bf16[2000,4096]{1,0:T(8,128)(2,1)} %get-tuple-element.17.refs_2_.refs_1_), custom_call_target="tpu_custom_call" | custom-call | flops 2147483648 | bytes 8388608 | tf_op jit(solution)/shard_map/first_lines/pallas_call | solution.py:678
  64.9 0.1 collective-permute-start
  65.0 5.0 %other_lines.1 = (f32[2,48,1024]{2,1,0:T(8,128)S(1)}, f32[2,48,1024]{2,1,0:T(8,128)S(1)}) custom-call(s32[1]{0:T(128)} %bitcast.core_ref, bf16[4096,256]{1,0:T(8,128)(2,1)S(1)} %get-tuple-element.20.refs_0_, bf16[2000,4096]{1,0:T(8,128)(2,1)} %get-tuple-element.17.refs_2_.refs_1_), custom_call_target="tpu_custom_call" | custom-call | flops 2046820352 | bytes 7995392 | tf_op jit(solution)/shard_map/other_lines/pallas_call | solution.py:678
  70.0 0.6 collective-permute-start.2
  70.6 0.0 collective-permute-done
  70.7 1.0 %collective-permute-start.1 = (bf16[48,1024]{1,0:T(8,128)(2,1)S(1)}, bf16[48,1024]{1,0:T(8,128)(2,1)S(1)}, u32[]{:S(2)}, u32[]{:S(2)}) collective-permute-start(bf16[48,1024]{1,0:T(8,128)(2,1)S(1)} %fusion.1), channel_id=1, source_target_pairs={{0,2},{1,3},{2,0},{3,1},{4,6},{5,7},{6,4},{7,5},{8,10},{9,11},{10,... | collective-permute-start | bytes 294920 | tf_op jit(solution)/shard_map/ppermute | solution.py:763
  71.6 0.3 collective-permute-done.2
  72.0 1.0 %collective-permute-start.3 = (bf16[48,1024]{1,0:T(8,128)(2,1)S(1)}, bf16[48,1024]{1,0:T(8,128)(2,1)S(1)}, u32[]{:S(2)}, u32[]{:S(2)}) collective-permute-start(bf16[48,1024]{1,0:T(8,128)(2,1)S(1)} %fusion.2), channel_id=1, source_target_pairs={{0,2},{1,3},{2,0},{3,1},{4,6},{5,7},{6,4},{7,5},{8,10},{9,11},{10,... | collective-permute-start | bytes 294920 | tf_op jit(solution)/shard_map/ppermute | solution.py:763
  73.0 3.0 %collective-permute-done.1 = bf16[48,1024]{1,0:T(8,128)(2,1)S(1)} collective-permute-done((bf16[48,1024]{1,0:T(8,128)(2,1)S(1)}, bf16[48,1024]{1,0:T(8,128)(2,1)S(1)}, u32[]{:S(2)}, u32[]{:S(2)}) %collective-permute-start.1) | collective-permute-done | bytes 98336 | tf_op jit(solution)/shard_map/ppermute | solution.py:763
  76.0 1.6 %collective-permute-done.3 = bf16[48,1024]{1,0:T(8,128)(2,1)S(1)} collective-permute-done((bf16[48,1024]{1,0:T(8,128)(2,1)S(1)}, bf16[48,1024]{1,0:T(8,128)(2,1)S(1)}, u32[]{:S(2)}, u32[]{:S(2)}) %collective-permute-start.3) | collective-permute-done | bytes 98336 | tf_op jit(solution)/shard_map/ppermute | solution.py:763
  77.6 0.8 fusion
  (6 shorter events, 0.2 us)
Async XLA Ops:
  1.6 14.3 %all-to-all-start = ((s32[32,1,128]{2,1,0:T(1,128)}), s32[32,1,128]{2,1,0:T(1,128)}, u32[]{:S(2)}, u32[]{:S(2)}) async-start(s32[32,1,128]{2,1,0:T(1,128)} %bitcast.22), calls=%async_computation | async-start | bytes 32768 | tf_op jit(solution)/shard_map/all_to_all | solution.py:724
  15.9 43.1 %all-to-all-start.1 = ((bf16[32,192,128]{2,1,0:T(8,128)(2,1)}), bf16[32,192,128]{2,1,0:T(8,128)(2,1)S(1)}, u32[]{:S(2)}, u32[]{:S(2)}) async-start(bf16[32,192,128]{2,1,0:T(8,128)(2,1)} %power.1), calls=%async_computation.1 | async-start | bytes 3145728 | tf_op jit(solution)/shard_map/all_to_all | solution.py:739
  64.9 5.6 %collective-permute-start = (f32[2,48,1024]{2,1,0:T(8,128)S(1)}, f32[2,48,1024]{2,1,0:T(8,128)S(1)}, u32[]{:S(2)}, u32[]{:S(2)}) collective-permute-start(f32[2,48,1024]{2,1,0:T(8,128)S(1)} %get-tuple-element.19), channel_id=1, source_target_pairs={{0,1},{1,0},{2,3},{3,2},{4,5},{5,4},{6,7},{7,6},{8,9},{9,8},{10,11... | collective-permute-start | bytes 1179656 | tf_op jit(solution)/shard_map/ppermute | solution.py:760
  70.0 1.9 %collective-permute-start.2 = (f32[2,48,1024]{2,1,0:T(8,128)S(1)}, f32[2,48,1024]{2,1,0:T(8,128)S(1)}, u32[]{:S(2)}, u32[]{:S(2)}) collective-permute-start(f32[2,48,1024]{2,1,0:T(8,128)S(1)} %get-tuple-element.22), channel_id=1, source_target_pairs={{0,1},{1,0},{2,3},{3,2},{4,5},{5,4},{6,7},{7,6},{8,9},{9,8},{10,11... | collective-permute-start | bytes 1179656 | tf_op jit(solution)/shard_map/ppermute | solution.py:760
  70.7 5.3 %collective-permute-start.1 = (bf16[48,1024]{1,0:T(8,128)(2,1)S(1)}, bf16[48,1024]{1,0:T(8,128)(2,1)S(1)}, u32[]{:S(2)}, u32[]{:S(2)}) collective-permute-start(bf16[48,1024]{1,0:T(8,128)(2,1)S(1)} %fusion.1), channel_id=1, source_target_pairs={{0,2},{1,3},{2,0},{3,1},{4,6},{5,7},{6,4},{7,5},{8,10},{9,11},{10,... | collective-permute-start | bytes 294920 | tf_op jit(solution)/shard_map/ppermute | solution.py:763
  72.0 5.6 %collective-permute-start.3 = (bf16[48,1024]{1,0:T(8,128)(2,1)S(1)}, bf16[48,1024]{1,0:T(8,128)(2,1)S(1)}, u32[]{:S(2)}, u32[]{:S(2)}) collective-permute-start(bf16[48,1024]{1,0:T(8,128)(2,1)S(1)} %fusion.2), channel_id=1, source_target_pairs={{0,2},{1,3},{2,0},{3,1},{4,6},{5,7},{6,4},{7,5},{8,10},{9,11},{10,... | collective-permute-start | bytes 294920 | tf_op jit(solution)/shard_map/ppermute | solution.py:763

commit v4 on v3

--- a/solution.py
+++ b/solution.py
@@ -248,16 +248,17 @@
 def power_kernel(
     tilt_table_ref,
     azimuth_table_ref,
+    perez_ref,
     *refs,
     n_line,
     n_bus,
     cap,
     rows,
 ):
-    sources = refs[:11]
-    out_ref = refs[11]
-    held = refs[12:23]
-    power_ref, dirint_rows, perez_rows, sems = refs[23:]
+    sources = refs[:10]
+    out_ref = refs[10]
+    held = refs[11:21]
+    power_ref, dirint_rows, sems = refs[21:]
     copies = [
         pltpu.make_async_copy(source, place, sems.at[i])
         for i, (source, place) in enumerate(zip(sources, held))
@@ -267,15 +268,13 @@
     for copy in copies:
         copy.wait()
     clear_all, cosz_all, sun_all, cell_all, sky_all = held[:5]
-    dirint_ref, perez_ref, tilt_class_ref, azimuth_class_ref, capacity_ref, slot_ref = held[5:]
+    dirint_ref, tilt_class_ref, azimuth_class_ref, capacity_ref, slot_ref = held[5:]
     n_hours, n_sites = clear_all.shape
     cells = dirint_ref.shape[0]
     dirint_rows[...] = jnp.zeros_like(dirint_rows)
     for begin in range(0, cells, LANES):
         count = min(LANES, cells - begin)
         dirint_rows[:, begin : begin + count] = dirint_ref[begin : begin + count].reshape(1, count)
-    perez_rows[...] = jnp.zeros_like(perez_rows)
-    perez_rows[: perez_ref.shape[0], : perez_ref.shape[1]] = perez_ref[...]
     tilt_class = tilt_class_ref[...]
     azimuth_class = azimuth_class_ref[...]
     tilt = jnp.zeros(tilt_class.shape, jnp.float32)
@@ -324,15 +323,12 @@
             direct = solar_constant * beam * coefficient
             diffuse = jnp.maximum(global_flat - direct * cosz, 0.1 * global_flat)
             bright = diffuse * airmass * (1.0 / solar_constant)
-            factor = [
-                jnp.take_along_axis(
-                    jnp.broadcast_to(perez_rows[row : row + 1, :], wide),
-                    sky,
-                    axis=1,
-                    mode="promise_in_bounds",
-                )
-                for row in range(6)
-            ]
+            factor = [jnp.full(wide, perez_ref[row, 0]) for row in range(6)]
+            for entry in range(1, perez_ref.shape[1]):
+                hit = sky == entry
+                factor = [
+                    jnp.where(hit, perez_ref[row, entry], factor[row]) for row in range(6)
+                ]
             circumsolar = jnp.maximum(0.0, factor[0] + factor[1] * bright + factor[2] * zenith)
             horizon = factor[3] + factor[4] * bright + factor[5] * zenith
             facing = jnp.maximum(
@@ -396,13 +392,12 @@
     owners = n_line * n_bus
     n_slots = n_line * cap
     cells = dirint_coef.shape[0]
-    rows = 32
+    rows = 64
     smem = pl.BlockSpec(memory_space=pltpu.SMEM)
     shape = (owners, n_slots * n_hours // LANES, LANES)
     operands = (
         *hourly,
         dirint_coef,
-        perez_coef,
         tilt_class.reshape(1, n_sites),
         azimuth_class.reshape(1, n_sites),
         capacity.reshape(1, n_sites),
@@ -411,13 +406,12 @@
     return pl.pallas_call(
         functools.partial(power_kernel, n_line=n_line, n_bus=n_bus, cap=cap, rows=rows),
         out_shape=jax.ShapeDtypeStruct(shape, jnp.bfloat16),
-        in_specs=[smem, smem] + [pl.BlockSpec(memory_space=pltpu.HBM)] * len(operands),
+        in_specs=[smem] * 3 + [pl.BlockSpec(memory_space=pltpu.HBM)] * len(operands),
         out_specs=pl.BlockSpec(memory_space=pltpu.VMEM),
         scratch_shapes=[pltpu.VMEM(x.shape, x.dtype) for x in operands]
         + [
             pltpu.VMEM((n_hours, n_sites), jnp.bfloat16),
             pltpu.VMEM((1, -(-cells // LANES) * LANES), jnp.float32),
-            pltpu.VMEM((8, LANES), jnp.float32),
             pltpu.SemaphoreType.DMA((len(operands),)),
         ],
         compiler_params=pltpu.CompilerParams(vmem_limit_bytes=64 << 20),
@@ -425,7 +419,7 @@
             flops=2 * 10**8, bytes_accessed=3 * 10**6, transcendentals=2 * 10**5
         ),
         name="power",
-    )(tilt_table, azimuth_table, *operands)
+    )(tilt_table, azimuth_table, perez_coef, *operands)
 
 
 def order_slots(tags_ref, sorted_ref, rank_ref, plan_ref, group_buses):
@@ -602,7 +596,7 @@
         )
         return carry
 
-    lax.fori_loop(0, n_groups, one, 0)
+    lax.fori_loop(0, n_groups, one, 0, unroll=2)
 
 
 def lines_kernel(

time: 78.7 us -> 78.6 us (level)
  starting transfers between devices: 15.1 us -> 16.9 us
  Pallas kernels: 55.6 us -> 54 us
    ppermute x2, starting transfers between devices: 1.93 us -> 3.28 us  [fast_device(): away = lax.ppermute(away, 'bus', other_chip)]
    ppermute x2, starting transfers between devices: 0.62 us -> 1.55 us  [fast_device(): summed = keep + lax.ppermute(send, 'bus', other_core)]
    pallas_call x2, Pallas kernels: 10.9 us -> 9.96 us  [lines(): pl.pallas_call(functools.partial(lines_kernel, cap=cap, begin=begin, coun...]
  transfers between devices with their start and end apart: 6 -> 6, of which waited for: 4 -> 3; matrix products, arithmetic and copies ran while one was open for 2% -> 2% of each run, Pallas kernels for 61% -> 61%
where the time goes in v4:
time: 78.6 us; the launch traced here: 78.1 us
  Pallas kernels  54 us (69%)
  starting transfers between devices  16.9 us (22%)
  waiting for transfers between devices  5.12 us (7%)
  local copies, waits for them, and re-layouts  1.02 us (1%)
  other arithmetic  0.97 us (1%)
    pallas_call x1, Pallas kernels, select_columns(): pl.pallas_call(functools.partial(select_kernel, group_buses=group_buses,...  36.8 us
    pallas_call x2, Pallas kernels, lines(): pl.pallas_call(functools.partial(lines_kernel, cap=cap, begin=begin, coun...  9.96 us
    all_to_all x1, starting transfers between devices, fast_device(): lax.all_to_all(tags, ('line', 'bus'), split_axis=0, concat_axis=0, tiled=...  7.43 us
    pallas_call x1, Pallas kernels, packed_power(): pl.pallas_call(functools.partial(power_kernel, n_line=n_line, n_bus=n_bus...  5.7 us
    all_to_all x1, starting transfers between devices, fast_device(): lax.all_to_all(outgoing, ('line', 'bus'), split_axis=0, concat_axis=0, ti...  4.6 us
    ppermute x2, waiting for transfers between devices, fast_device(): away = lax.ppermute(away, 'bus', other_chip)  3.94 us
    ppermute x2, starting transfers between devices, fast_device(): away = lax.ppermute(away, 'bus', other_chip)  3.28 us
    pallas_call x1, Pallas kernels, place_sites(): pl.pallas_call(functools.partial(place_kernel, owners=owners, group_buses...  1.6 us
  transfers between devices with their start and end apart: 6, of which 3 were waited for; matrix products, arithmetic and copies ran while one was open for 2% of the time, Pallas kernels for 61%

profile of v4, /device:TPU:0, one launch (start us, length us, event | category | flops | bytes accessed | tf_op | source)
XLA Modules:
  0.0 78.1 jit_solution(12959137932020238988)
XLA Ops:
  0.0 1.6 %place.1 = (s32[1,256]{1,0:T(1,128)}, s32[32,128]{1,0:T(8,128)}) custom-call(s32[1,256]{1,0:T(1,128)} %bitcast.26), custom_call_target="tpu_custom_call" | custom-call | flops 1000000 | bytes 100000 | tf_op jit(solution)/shard_map/place/pallas_call | solution.py:230
  1.6 7.4 %all-to-all-start = ((s32[32,1,128]{2,1,0:T(1,128)}), s32[32,1,128]{2,1,0:T(1,128)}, u32[]{:S(2)}, u32[]{:S(2)}) async-start(s32[32,1,128]{2,1,0:T(1,128)} %bitcast.22), calls=%async_computation | async-start | bytes 32768 | tf_op jit(solution)/shard_map/all_to_all | solution.py:718
  9.0 5.7 %power.1 = bf16[32,192,128]{2,1,0:T(8,128)(2,1)} custom-call(f32[8]{0:T(128)} %tilt_table_ref.1, f32[12]{0:T(128)} %azimuth_table_ref.1, f32[6,8]{1,0:T(8,128)} %perez_ref.1, f32[192,256]{1,0:T(8,128)} %refs_0_.1, f32[192,256]{1,0:T(8,128)} %refs_1_.1, f32[192,256]{1,0:T(8,128)} %refs_2_.1, s32[192,256]{1,0:T(8,128)} %refs_3_.1, s32[192,256]{1,0:T(8,128)} %refs_4_.1, ...), custom_call_target="tpu_custom_call" | custom-call | flops 200000000 | bytes 3000000 | tf_op jit(solution)/shard_map/power/pallas_call | solution.py:406
  14.8 1.2 %all-to-all-done = s32[32,1,128]{2,1,0:T(1,128)} async-done(((s32[32,1,128]{2,1,0:T(1,128)}), s32[32,1,128]{2,1,0:T(1,128)}, u32[]{:S(2)}, u32[]{:S(2)}) %all-to-all-start) | async-done | bytes 16416 | tf_op jit(solution)/shard_map/all_to_all | solution.py:718
  15.9 4.6 %all-to-all-start.1 = ((bf16[32,192,128]{2,1,0:T(8,128)(2,1)}), bf16[32,192,128]{2,1,0:T(8,128)(2,1)S(1)}, u32[]{:S(2)}, u32[]{:S(2)}) async-start(bf16[32,192,128]{2,1,0:T(8,128)(2,1)} %power.1), calls=%async_computation.1 | async-start | bytes 3145728 | tf_op jit(solution)/shard_map/all_to_all | solution.py:733
  20.5 0.8 %copy.19 = s32[32,1,128]{0,2,1:T(8,128)S(1)} copy(s32[32,1,128]{2,1,0:T(1,128)} %all-to-all-done) | data formatting | bytes 32768 | tf_op jit(solution)/shard_map/all_to_all | solution.py:718
  21.4 0.1 copy.20
  21.5 0.1 reshape.37.tags_ref
  21.6 36.8 %select.7 = (bf16[2000,4096]{1,0:T(8,128)(2,1)}, s32[8,512]{1,0:T(8,128)S(1)}) custom-call(s32[8,512]{1,0:T(8,128)S(1)} %reshape.37.tags_ref, bf16[2000,17536]{1,0:T(8,128)(2,1)} %factors_ref.1), custom_call_target="tpu_custom_call" | custom-call | flops 37748736000 | bytes 73728000 | tf_op jit(solution)/shard_map/select/pallas_call | solution.py:550
  58.3 0.0 all-to-all-done.1.refs_1_
  58.3 5.0 %first_lines.1 = (f32[2,48,1024]{2,1,0:T(8,128)S(1)}, f32[2,48,1024]{2,1,0:T(8,128)S(1)}, bf16[4096,256]{1,0:T(8,128)(2,1)S(1)}) custom-call(s32[1]{0:T(128)} %bitcast.core_ref, s32[8,512]{1,0:T(8,128)S(1)} %get-tuple-element.15.refs_0_, bf16[32,192,128]{2,1,0:T(8,128)(2,1)S(1)} %all-to-all-done.1.refs_1_, bf16[2000,4096]{1,0:T(8,128)(2,1)} %get-tuple-element.17.refs_2_.refs_1_), custom_call_target="tpu_custom_call" | custom-call | flops 2147483648 | bytes 8388608 | tf_op jit(solution)/shard_map/first_lines/pallas_call | solution.py:672
  63.3 1.5 %collective-permute-start = (f32[2,48,1024]{2,1,0:T(8,128)S(1)}, f32[2,48,1024]{2,1,0:T(8,128)S(1)}, u32[]{:S(2)}, u32[]{:S(2)}) collective-permute-start(f32[2,48,1024]{2,1,0:T(8,128)S(1)} %get-tuple-element.19), channel_id=1, source_target_pairs={{0,1},{1,0},{2,3},{3,2},{4,5},{5,4},{6,7},{7,6},{8,9},{9,8},{10,11... | collective-permute-start | bytes 1179656 | tf_op jit(solution)/shard_map/ppermute | solution.py:754
  64.8 5.0 %other_lines.1 = (f32[2,48,1024]{2,1,0:T(8,128)S(1)}, f32[2,48,1024]{2,1,0:T(8,128)S(1)}) custom-call(s32[1]{0:T(128)} %bitcast.core_ref, bf16[4096,256]{1,0:T(8,128)(2,1)S(1)} %get-tuple-element.20.refs_0_, bf16[2000,4096]{1,0:T(8,128)(2,1)} %get-tuple-element.17.refs_2_.refs_1_), custom_call_target="tpu_custom_call" | custom-call | flops 2046820352 | bytes 7995392 | tf_op jit(solution)/shard_map/other_lines/pallas_call | solution.py:672
  69.8 0.1 collective-permute-start.2
  69.9 0.0 collective-permute-done
  70.0 1.7 %collective-permute-start.1 = (bf16[48,1024]{1,0:T(8,128)(2,1)S(1)}, bf16[48,1024]{1,0:T(8,128)(2,1)S(1)}, u32[]{:S(2)}, u32[]{:S(2)}) collective-permute-start(bf16[48,1024]{1,0:T(8,128)(2,1)S(1)} %fusion.1), channel_id=1, source_target_pairs={{0,2},{1,3},{2,0},{3,1},{4,6},{5,7},{6,4},{7,5},{8,10},{9,11},{10,... | collective-permute-start | bytes 294920 | tf_op jit(solution)/shard_map/ppermute | solution.py:757
  71.7 0.0 collective-permute-done.2
  71.8 1.6 %collective-permute-start.3 = (bf16[48,1024]{1,0:T(8,128)(2,1)S(1)}, bf16[48,1024]{1,0:T(8,128)(2,1)S(1)}, u32[]{:S(2)}, u32[]{:S(2)}) collective-permute-start(bf16[48,1024]{1,0:T(8,128)(2,1)S(1)} %fusion.2), channel_id=1, source_target_pairs={{0,2},{1,3},{2,0},{3,1},{4,6},{5,7},{6,4},{7,5},{8,10},{9,11},{10,... | collective-permute-start | bytes 294920 | tf_op jit(solution)/shard_map/ppermute | solution.py:757
  73.3 2.3 %collective-permute-done.1 = bf16[48,1024]{1,0:T(8,128)(2,1)S(1)} collective-permute-done((bf16[48,1024]{1,0:T(8,128)(2,1)S(1)}, bf16[48,1024]{1,0:T(8,128)(2,1)S(1)}, u32[]{:S(2)}, u32[]{:S(2)}) %collective-permute-start.1) | collective-permute-done | bytes 98336 | tf_op jit(solution)/shard_map/ppermute | solution.py:757
  75.7 1.6 %collective-permute-done.3 = bf16[48,1024]{1,0:T(8,128)(2,1)S(1)} collective-permute-done((bf16[48,1024]{1,0:T(8,128)(2,1)S(1)}, bf16[48,1024]{1,0:T(8,128)(2,1)S(1)}, u32[]{:S(2)}, u32[]{:S(2)}) %collective-permute-start.3) | collective-permute-done | bytes 98336 | tf_op jit(solution)/shard_map/ppermute | solution.py:757
  77.4 0.8 fusion
  (6 shorter events, 0.2 us)
Async XLA Ops:
  1.6 14.3 %all-to-all-start = ((s32[32,1,128]{2,1,0:T(1,128)}), s32[32,1,128]{2,1,0:T(1,128)}, u32[]{:S(2)}, u32[]{:S(2)}) async-start(s32[32,1,128]{2,1,0:T(1,128)} %bitcast.22), calls=%async_computation | async-start | bytes 32768 | tf_op jit(solution)/shard_map/all_to_all | solution.py:718
  15.9 42.4 %all-to-all-start.1 = ((bf16[32,192,128]{2,1,0:T(8,128)(2,1)}), bf16[32,192,128]{2,1,0:T(8,128)(2,1)S(1)}, u32[]{:S(2)}, u32[]{:S(2)}) async-start(bf16[32,192,128]{2,1,0:T(8,128)(2,1)} %power.1), calls=%async_computation.1 | async-start | bytes 3145728 | tf_op jit(solution)/shard_map/all_to_all | solution.py:733
  63.3 6.6 %collective-permute-start = (f32[2,48,1024]{2,1,0:T(8,128)S(1)}, f32[2,48,1024]{2,1,0:T(8,128)S(1)}, u32[]{:S(2)}, u32[]{:S(2)}) collective-permute-start(f32[2,48,1024]{2,1,0:T(8,128)S(1)} %get-tuple-element.19), channel_id=1, source_target_pairs={{0,1},{1,0},{2,3},{3,2},{4,5},{5,4},{6,7},{7,6},{8,9},{9,8},{10,11... | collective-permute-start | bytes 1179656 | tf_op jit(solution)/shard_map/ppermute | solution.py:754
  69.8 1.9 %collective-permute-start.2 = (f32[2,48,1024]{2,1,0:T(8,128)S(1)}, f32[2,48,1024]{2,1,0:T(8,128)S(1)}, u32[]{:S(2)}, u32[]{:S(2)}) collective-permute-start(f32[2,48,1024]{2,1,0:T(8,128)S(1)} %get-tuple-element.22), channel_id=1, source_target_pairs={{0,1},{1,0},{2,3},{3,2},{4,5},{5,4},{6,7},{7,6},{8,9},{9,8},{10,11... | collective-permute-start | bytes 1179656 | tf_op jit(solution)/shard_map/ppermute | solution.py:754
  70.0 5.7 %collective-permute-start.1 = (bf16[48,1024]{1,0:T(8,128)(2,1)S(1)}, bf16[48,1024]{1,0:T(8,128)(2,1)S(1)}, u32[]{:S(2)}, u32[]{:S(2)}) collective-permute-start(bf16[48,1024]{1,0:T(8,128)(2,1)S(1)} %fusion.1), channel_id=1, source_target_pairs={{0,2},{1,3},{2,0},{3,1},{4,6},{5,7},{6,4},{7,5},{8,10},{9,11},{10,... | collective-permute-start | bytes 294920 | tf_op jit(solution)/shard_map/ppermute | solution.py:757
  71.8 5.6 %collective-permute-start.3 = (bf16[48,1024]{1,0:T(8,128)(2,1)S(1)}, bf16[48,1024]{1,0:T(8,128)(2,1)S(1)}, u32[]{:S(2)}, u32[]{:S(2)}) collective-permute-start(bf16[48,1024]{1,0:T(8,128)(2,1)S(1)} %fusion.2), channel_id=1, source_target_pairs={{0,2},{1,3},{2,0},{3,1},{4,6},{5,7},{6,4},{7,5},{8,10},{9,11},{10,... | collective-permute-start | bytes 294920 | tf_op jit(solution)/shard_map/ppermute | solution.py:757

commit v5 on v4

--- a/solution.py
+++ b/solution.py
@@ -654,7 +654,8 @@
             even = turned[low : low + rows_each]
             odd = turned[low + rows_each : low + 2 * rows_each]
             keep_ref[x, :, pl.ds(at, block)] = jnp.where(core_zero, even, odd)
-            send_ref[x, :, pl.ds(at, block)] = jnp.where(core_zero, odd, even)
+            away = jnp.where(core_zero, odd, even)
+            send_ref[x, :, pl.ds(at, block)] = away.astype(jnp.bfloat16)
         return carry
 
     lax.fori_loop(0, n_blocks, one, 0)
@@ -667,13 +668,14 @@
     vmem = pl.BlockSpec(memory_space=pltpu.VMEM)
     hbm = pl.BlockSpec(memory_space=pltpu.HBM)
     part = jax.ShapeDtypeStruct(shape + (padded,), jnp.float32)
+    sent = jax.ShapeDtypeStruct(shape + (padded,), jnp.bfloat16)
     moved = jax.ShapeDtypeStruct(moved_shape, jnp.bfloat16)
     block = 512
     return pl.pallas_call(
         functools.partial(lines_kernel, cap=cap, begin=begin, count=count, first=first),
         in_specs=[smem] + ([vmem, vmem] if first else [hbm]) + [hbm],
         out_specs=[vmem, vmem] + ([hbm] if first else []),
-        out_shape=[part, part] + ([moved] if first else []),
+        out_shape=[part, sent] + ([moved] if first else []),
         scratch_shapes=[
             pltpu.VMEM(moved_shape, jnp.bfloat16),
             pltpu.VMEM((padded, picked.shape[1]), jnp.bfloat16),
@@ -751,7 +753,7 @@
     )
     ends = []
     for keep, send in ((keep_a, send_a), (keep_b, send_b)):
-        summed = keep + lax.ppermute(send, "bus", other_core)
+        summed = keep + lax.ppermute(send, "bus", other_core).astype(jnp.float32)
         own = jnp.where(near, summed[0], summed[1])
         away = jnp.where(near, summed[1], summed[0]).astype(jnp.bfloat16)
         away = lax.ppermute(away, "bus", other_chip)

time: 78.6 us -> 80.5 us (1.024)
  local copies, waits for them, and re-layouts: 1.02 us -> 3.94 us
  starting transfers between devices: 16.9 us -> 15.1 us
    unnamed x0 -> x4, local copies, waits for them, and re-layouts: none -> 2.92 us
    ppermute x2, starting transfers between devices: 1.55 us -> 0.58 us  [fast_device(): summed = keep + lax.ppermute(send, 'bus', other_core).astype(jnp.float32)]
  transfers between devices with their start and end apart: 6 -> 6, of which waited for: 3 -> 3; matrix products, arithmetic and copies ran while one was open for 2% -> 1% of each run, Pallas kernels for 61% -> 60%
where the time goes in v5:
time: 80.5 us; the launch traced here: 79.9 us
  Pallas kernels  54.3 us (67%)
  starting transfers between devices  15.1 us (19%)
  waiting for transfers between devices  5.44 us (7%)
  local copies, waits for them, and re-layouts  3.94 us (5%)
  other arithmetic  0.96 us (1%)
    pallas_call x1, Pallas kernels, select_columns(): pl.pallas_call(functools.partial(select_kernel, group_buses=group_buses,...  37 us
    pallas_call x2, Pallas kernels, lines(): pl.pallas_call(functools.partial(lines_kernel, cap=cap, begin=begin, coun...  9.96 us
    all_to_all x1, starting transfers between devices, fast_device(): lax.all_to_all(tags, ('line', 'bus'), split_axis=0, concat_axis=0, tiled=...  7.43 us
    pallas_call x1, Pallas kernels, packed_power(): pl.pallas_call(functools.partial(power_kernel, n_line=n_line, n_bus=n_bus...  5.71 us
    all_to_all x1, starting transfers between devices, fast_device(): lax.all_to_all(outgoing, ('line', 'bus'), split_axis=0, concat_axis=0, ti...  4.46 us
    ppermute x2, waiting for transfers between devices, fast_device(): away = lax.ppermute(away, 'bus', other_chip)  4.12 us
    unnamed x4, local copies, waits for them, and re-layouts  2.92 us
    ppermute x2, starting transfers between devices, fast_device(): away = lax.ppermute(away, 'bus', other_chip)  2.66 us
  transfers between devices with their start and end apart: 6, of which 3 were waited for; matrix products, arithmetic and copies ran while one was open for 1% of the time, Pallas kernels for 60%

profile of v5, /device:TPU:0, one launch (start us, length us, event | category | flops | bytes accessed | tf_op | source)
XLA Modules:
  0.0 79.9 jit_solution(5198338731096900466)
XLA Ops:
  0.0 1.6 %place.1 = (s32[1,256]{1,0:T(1,128)}, s32[32,128]{1,0:T(8,128)}) custom-call(s32[1,256]{1,0:T(1,128)} %bitcast.26), custom_call_target="tpu_custom_call" | custom-call | flops 1000000 | bytes 100000 | tf_op jit(solution)/shard_map/place/pallas_call | solution.py:230
  1.6 7.4 %all-to-all-start = ((s32[32,1,128]{2,1,0:T(1,128)}), s32[32,1,128]{2,1,0:T(1,128)}, u32[]{:S(2)}, u32[]{:S(2)}) async-start(s32[32,1,128]{2,1,0:T(1,128)} %bitcast.22), calls=%async_computation | async-start | bytes 32768 | tf_op jit(solution)/shard_map/all_to_all | solution.py:720
  9.0 5.7 %power.1 = bf16[32,192,128]{2,1,0:T(8,128)(2,1)} custom-call(f32[8]{0:T(128)} %tilt_table_ref.1, f32[12]{0:T(128)} %azimuth_table_ref.1, f32[6,8]{1,0:T(8,128)} %perez_ref.1, f32[192,256]{1,0:T(8,128)} %refs_0_.1, f32[192,256]{1,0:T(8,128)} %refs_1_.1, f32[192,256]{1,0:T(8,128)} %refs_2_.1, s32[192,256]{1,0:T(8,128)} %refs_3_.1, s32[192,256]{1,0:T(8,128)} %refs_4_.1, ...), custom_call_target="tpu_custom_call" | custom-call | flops 200000000 | bytes 3000000 | tf_op jit(solution)/shard_map/power/pallas_call | solution.py:406
  14.8 1.3 %all-to-all-done = s32[32,1,128]{2,1,0:T(1,128)} async-done(((s32[32,1,128]{2,1,0:T(1,128)}), s32[32,1,128]{2,1,0:T(1,128)}, u32[]{:S(2)}, u32[]{:S(2)}) %all-to-all-start) | async-done | bytes 16416 | tf_op jit(solution)/shard_map/all_to_all | solution.py:720
  16.1 4.5 %all-to-all-start.1 = ((bf16[32,192,128]{2,1,0:T(8,128)(2,1)}), bf16[32,192,128]{2,1,0:T(8,128)(2,1)S(1)}, u32[]{:S(2)}, u32[]{:S(2)}) async-start(bf16[32,192,128]{2,1,0:T(8,128)(2,1)} %power.1), calls=%async_computation.1 | async-start | bytes 3145728 | tf_op jit(solution)/shard_map/all_to_all | solution.py:735
  20.6 0.8 %copy.19 = s32[32,1,128]{0,2,1:T(8,128)S(1)} copy(s32[32,1,128]{2,1,0:T(1,128)} %all-to-all-done) | data formatting | bytes 32768 | tf_op jit(solution)/shard_map/all_to_all | solution.py:720
  21.4 0.1 copy.20
  21.5 0.1 reshape.37.tags_ref
  21.6 37.0 %select.7 = (bf16[2000,4096]{1,0:T(8,128)(2,1)}, s32[8,512]{1,0:T(8,128)S(1)}) custom-call(s32[8,512]{1,0:T(8,128)S(1)} %reshape.37.tags_ref, bf16[2000,17536]{1,0:T(8,128)(2,1)} %factors_ref.1), custom_call_target="tpu_custom_call" | custom-call | flops 37748736000 | bytes 73728000 | tf_op jit(solution)/shard_map/select/pallas_call | solution.py:550
  58.6 0.0 all-to-all-done.1.refs_1_
  58.6 5.0 %first_lines.1 = (f32[2,48,1024]{2,1,0:T(8,128)S(1)}, bf16[2,48,1024]{2,1,0:T(8,128)(2,1)S(1)}, bf16[4096,256]{1,0:T(8,128)(2,1)S(1)}) custom-call(s32[1]{0:T(128)} %bitcast.core_ref, s32[8,512]{1,0:T(8,128)S(1)} %get-tuple-element.15.refs_0_, bf16[32,192,128]{2,1,0:T(8,128)(2,1)S(1)} %all-to-all-done.1.refs_1_, ...), custom_call_target="tpu_custom_call" | custom-call | flops 2147483648 | bytes 8388608 | tf_op jit(solution)/shard_map/first_lines/pallas_call | solution.py:674
  63.6 0.0 copy-start
  63.6 1.3 %copy-done = bf16[4096,256]{1,0:T(8,128)(2,1)} copy-done((bf16[4096,256]{1,0:T(8,128)(2,1)}, bf16[4096,256]{1,0:T(8,128)(2,1)S(1)}, u32[]{:S(2)}) %copy-start) | copy-done | bytes 2097176
  65.0 0.0 collective-permute-start
  65.0 1.6 %copy-done.1 = bf16[4096,256]{1,0:T(8,128)(2,1)S(1)} copy-done((bf16[4096,256]{1,0:T(8,128)(2,1)S(1)}, bf16[4096,256]{1,0:T(8,128)(2,1)}, u32[]{:S(2)}) %copy-start.1) | copy-done | bytes 2097176
  66.6 5.0 %other_lines.1 = (f32[2,48,1024]{2,1,0:T(8,128)S(1)}, bf16[2,48,1024]{2,1,0:T(8,128)(2,1)S(1)}) custom-call(s32[1]{0:T(128)} %bitcast.core_ref, bf16[4096,256]{1,0:T(8,128)(2,1)S(1)} %copy-done.1, bf16[2000,4096]{1,0:T(8,128)(2,1)} %get-tuple-element.17.refs_2_.refs_1_), custom_call_target="tpu_custom_call" | custom-call | flops 2046820352 | bytes 7995392 | tf_op jit(solution)/shard_map/other_lines/pallas_call | solution.py:674
  71.6 0.6 collective-permute-start.2
  72.1 0.0 collective-permute-done
  72.2 1.3 %collective-permute-start.1 = (bf16[48,1024]{1,0:T(8,128)(2,1)S(1)}, bf16[48,1024]{1,0:T(8,128)(2,1)S(1)}, u32[]{:S(2)}, u32[]{:S(2)}) collective-permute-start(bf16[48,1024]{1,0:T(8,128)(2,1)S(1)} %fusion.1), channel_id=1, source_target_pairs={{0,2},{1,3},{2,0},{3,1},{4,6},{5,7},{6,4},{7,5},{8,10},{9,11},{10,... | collective-permute-start | bytes 294920 | tf_op jit(solution)/shard_map/ppermute | solution.py:759
  73.5 0.0 collective-permute-done.2
  73.6 1.3 %collective-permute-start.3 = (bf16[48,1024]{1,0:T(8,128)(2,1)S(1)}, bf16[48,1024]{1,0:T(8,128)(2,1)S(1)}, u32[]{:S(2)}, u32[]{:S(2)}) collective-permute-start(bf16[48,1024]{1,0:T(8,128)(2,1)S(1)} %fusion.2), channel_id=1, source_target_pairs={{0,2},{1,3},{2,0},{3,1},{4,6},{5,7},{6,4},{7,5},{8,10},{9,11},{10,... | collective-permute-start | bytes 294920 | tf_op jit(solution)/shard_map/ppermute | solution.py:759
  75.0 2.6 %collective-permute-done.1 = bf16[48,1024]{1,0:T(8,128)(2,1)S(1)} collective-permute-done((bf16[48,1024]{1,0:T(8,128)(2,1)S(1)}, bf16[48,1024]{1,0:T(8,128)(2,1)S(1)}, u32[]{:S(2)}, u32[]{:S(2)}) %collective-permute-start.1) | collective-permute-done | bytes 98336 | tf_op jit(solution)/shard_map/ppermute | solution.py:759
  77.6 1.5 %collective-permute-done.3 = bf16[48,1024]{1,0:T(8,128)(2,1)S(1)} collective-permute-done((bf16[48,1024]{1,0:T(8,128)(2,1)S(1)}, bf16[48,1024]{1,0:T(8,128)(2,1)S(1)}, u32[]{:S(2)}, u32[]{:S(2)}) %collective-permute-start.3) | collective-permute-done | bytes 98336 | tf_op jit(solution)/shard_map/ppermute | solution.py:759
  79.1 0.8 fusion
  (7 shorter events, 0.2 us)
Async XLA Ops:
  1.6 14.5 %all-to-all-start = ((s32[32,1,128]{2,1,0:T(1,128)}), s32[32,1,128]{2,1,0:T(1,128)}, u32[]{:S(2)}, u32[]{:S(2)}) async-start(s32[32,1,128]{2,1,0:T(1,128)} %bitcast.22), calls=%async_computation | async-start | bytes 32768 | tf_op jit(solution)/shard_map/all_to_all | solution.py:720
  16.1 42.6 %all-to-all-start.1 = ((bf16[32,192,128]{2,1,0:T(8,128)(2,1)}), bf16[32,192,128]{2,1,0:T(8,128)(2,1)S(1)}, u32[]{:S(2)}, u32[]{:S(2)}) async-start(bf16[32,192,128]{2,1,0:T(8,128)(2,1)} %power.1), calls=%async_computation.1 | async-start | bytes 3145728 | tf_op jit(solution)/shard_map/all_to_all | solution.py:735
  63.6 1.3 %copy-start = (bf16[4096,256]{1,0:T(8,128)(2,1)}, bf16[4096,256]{1,0:T(8,128)(2,1)S(1)}, u32[]{:S(2)}) copy-start(bf16[4096,256]{1,0:T(8,128)(2,1)S(1)} %get-tuple-element.20.refs_0_) | copy-start | bytes 6291460
  65.0 7.2 %collective-permute-start = (bf16[2,48,1024]{2,1,0:T(8,128)(2,1)S(1)}, bf16[2,48,1024]{2,1,0:T(8,128)(2,1)S(1)}, u32[]{:S(2)}, u32[]{:S(2)}) collective-permute-start(bf16[2,48,1024]{2,1,0:T(8,128)(2,1)S(1)} %get-tuple-element.19), channel_id=1, source_target_pairs={{0,1},{1,0},{2,3},{3,2},{4,5},{5,4},{6,7},{7,6},{8,9},{9,8},{10,11... | collective-permute-start | bytes 589832 | tf_op jit(solution)/shard_map/ppermute | solution.py:756
  65.0 1.6 %copy-start.1 = (bf16[4096,256]{1,0:T(8,128)(2,1)S(1)}, bf16[4096,256]{1,0:T(8,128)(2,1)}, u32[]{:S(2)}) copy-start(bf16[4096,256]{1,0:T(8,128)(2,1)} %copy-done) | copy-start | bytes 6291460
  71.6 2.0 %collective-permute-start.2 = (bf16[2,48,1024]{2,1,0:T(8,128)(2,1)S(1)}, bf16[2,48,1024]{2,1,0:T(8,128)(2,1)S(1)}, u32[]{:S(2)}, u32[]{:S(2)}) collective-permute-start(bf16[2,48,1024]{2,1,0:T(8,128)(2,1)S(1)} %get-tuple-element.22), channel_id=1, source_target_pairs={{0,1},{1,0},{2,3},{3,2},{4,5},{5,4},{6,7},{7,6},{8,9},{9,8},{10,11... | collective-permute-start | bytes 589832 | tf_op jit(solution)/shard_map/ppermute | solution.py:756
  72.2 5.4 %collective-permute-start.1 = (bf16[48,1024]{1,0:T(8,128)(2,1)S(1)}, bf16[48,1024]{1,0:T(8,128)(2,1)S(1)}, u32[]{:S(2)}, u32[]{:S(2)}) collective-permute-start(bf16[48,1024]{1,0:T(8,128)(2,1)S(1)} %fusion.1), channel_id=1, source_target_pairs={{0,2},{1,3},{2,0},{3,1},{4,6},{5,7},{6,4},{7,5},{8,10},{9,11},{10,... | collective-permute-start | bytes 294920 | tf_op jit(solution)/shard_map/ppermute | solution.py:759
  73.6 5.5 %collective-permute-start.3 = (bf16[48,1024]{1,0:T(8,128)(2,1)S(1)}, bf16[48,1024]{1,0:T(8,128)(2,1)S(1)}, u32[]{:S(2)}, u32[]{:S(2)}) collective-permute-start(bf16[48,1024]{1,0:T(8,128)(2,1)S(1)} %fusion.2), channel_id=1, source_target_pairs={{0,2},{1,3},{2,0},{3,1},{4,6},{5,7},{6,4},{7,5},{8,10},{9,11},{10,... | collective-permute-start | bytes 294920 | tf_op jit(solution)/shard_map/ppermute | solution.py:759
